TPU v7x, 32 devices: a whole 2x2x4 slice. The times are simulated.
32 devices in a mesh: ctx: 16 (over z, y, core), fsdp: 2 (over x).
Axes of the slice: x: 2, y: 2, z: 4, core: 2. Of those that a mesh axis runs over, the one named last changes fastest.
Arguments:
- tokens: bfloat16 [2, 2, 8192, 768], P(None, 'fsdp', 'ctx'), may hold values from -6 to 6
- cotangent: bfloat16 [2, 2, 8192, 768], P(None, 'fsdp', 'ctx'), may hold values from -6 to 6
- doc_lengths: int32 [2, 2, 8], P(None, 'fsdp'), may hold values from 1 to 4096, 8192 in all within a row
- gain_attn: bfloat16 [768], P('fsdp'), may hold values from 0.25 to 1.75
- w_query: bfloat16 [768, 768], P('fsdp'), may hold values from -0.21875 to 0.21875
- w_key: bfloat16 [768, 768], P('fsdp'), may hold values from -0.21875 to 0.21875
- w_value: bfloat16 [768, 768], P('fsdp'), may hold values from -0.21875 to 0.21875
- w_out: bfloat16 [768, 768], P('fsdp'), may hold values from -2.5 to 2.5
- gain_mlp: bfloat16 [768], P('fsdp'), may hold values from 0.25 to 1.75
- w_gate: bfloat16 [768, 2048], P('fsdp'), may hold values from -0.21875 to 0.21875
- w_up: bfloat16 [768, 2048], P('fsdp'), may hold values from -0.21875 to 0.21875
- w_down: bfloat16 [2048, 768], P('fsdp'), may hold values from -0.125 to 0.125
Outputs:
- output: bfloat16 [2, 2, 8192, 768], P(None, 'fsdp', 'ctx')
- grad_tokens: bfloat16 [2, 2, 8192, 768], P(None, 'fsdp', 'ctx')
- grad_gain_attn: float32 [768], P('fsdp')
- grad_w_query: float32 [768, 768], P('fsdp')
- grad_w_key: float32 [768, 768], P('fsdp')
- grad_w_value: float32 [768, 768], P('fsdp')
- grad_w_out: float32 [768, 768], P('fsdp')
- grad_gain_mlp: float32 [768], P('fsdp')
- grad_w_gate: float32 [768, 2048], P('fsdp')
- grad_w_up: float32 [768, 2048], P('fsdp')
- grad_w_down: float32 [2048, 768], P('fsdp')
Inputs may be any that keep to these rules, and one draw needn't show every extreme that they name: `doc_lengths`: each row holds the lengths of the 8 documents of one stream, summing to 8192; the longest is exactly 4096.
All inputs are finite; a program needn't handle non-finite values.
Results may differ from a plain program's by a relative error of at most 0.024.
Values may be sent and summed in bfloat16 or wider, within the bound.
A program may use at most 88 MiB of HBM per device.

v0:
```python
import jax
import jax.numpy as jnp
from jax import lax
from jax.sharding import PartitionSpec as P

HEAD_DIM = 64
DOC_MAX = 4096


EPS = 1e-05
NEG = -1e30


def shifted(value, axis, steps):
    count = lax.axis_size(axis)
    initial, last = (max(0, -steps), min(count, count - steps))
    return lax.ppermute(value, axis, [(source, source + steps) for source in range(initial, last)])


def shifted_2(shard, axis, by):
    size = lax.axis_size(axis)
    return lax.ppermute(shard, axis, [(i, (i + by) % size) for i in range(size)])


def shortened(shard):
    return jax.tree.map(lambda a: a.astype(jnp.bfloat16) if a.dtype == jnp.float32 else a, shard)


def norm_forward(values, gain):
    recip_rows = lax.rsqrt(jnp.mean(values * values, -1, keepdims=True) + EPS)
    return (values * recip_rows * gain, recip_rows)


def norm_backward(grad_out, values, recip_rows, gain):
    scaled = grad_out * gain
    grad_in = recip_rows * scaled - values * (recip_rows * recip_rows * recip_rows) * jnp.mean(
        scaled * values, -1, keepdims=True
    )
    return (grad_in, jnp.sum(grad_out * values * recip_rows, 0))


def rotary_tables(offsets, head_dim):
    half_dim = head_dim // 2
    inverse = jnp.power(10000.0, -jnp.arange(half_dim, dtype=jnp.float32) / half_dim)
    angles = offsets.astype(jnp.float32)[:, None] * inverse[None, :]
    cos_table = jnp.cos(angles)
    sine_table = jnp.sin(angles)
    return (
        jnp.concatenate([cos_table, cos_table], -1)[:, None, :],
        jnp.concatenate([sine_table, sine_table], -1)[:, None, :],
    )


def rotate(values, cos_table, sine_table):
    half_dim = values.shape[-1] // 2
    turned = jnp.concatenate([-values[..., half_dim:], values[..., :half_dim]], -1)
    return values * cos_table + turned * sine_table


def rotate_back(grads, cos_table, sine_table):
    half_dim = grads.shape[-1] // 2
    scaled = grads * sine_table
    turned = jnp.concatenate([scaled[..., half_dim:], -scaled[..., :half_dim]], -1)
    return grads * cos_table + turned


def document_starts(lengths, positions):
    doc_ends = jnp.cumsum(lengths)
    doc_begins = doc_ends - lengths
    inside = (positions[:, None] >= doc_begins[None, :]) & (positions[:, None] < doc_ends[None, :])
    return jnp.sum(jnp.where(inside, doc_begins[None, :], 0), -1)


def block_scores(queries, key_block, key_first, query_pos, begins, score_scale):
    raw_scores = (
        jnp.einsum("qhd,khd->hqk", queries, key_block, preferred_element_type=jnp.float32)
        * score_scale
    )
    key_pos = key_first + jnp.arange(key_block.shape[0], dtype=jnp.int32)
    key_valid = (key_pos[None, :] >= begins[:, None]) & (key_pos[None, :] <= query_pos[:, None])
    return jnp.where(key_valid[None], raw_scores, NEG)


def micro_step(gathered, tokens, cotangent, lengths):
    gain_attn, w_query, w_key, w_value, w_out, gain_mlp, w_gate, w_up, w_down = gathered
    tok_rows = tokens.shape[0]
    model_width = tokens.shape[1]
    head_count = model_width // HEAD_DIM
    score_scale = HEAD_DIM ** (-0.5)
    back_span = (DOC_MAX - 2) // tok_rows + 1
    cycle_place = lax.axis_index("ctx")
    query_pos = cycle_place * tok_rows + jnp.arange(tok_rows, dtype=jnp.int32)
    begins = document_starts(lengths, query_pos)
    lowest = jnp.min(begins)
    cos_table, sine_table = rotary_tables(query_pos - begins, HEAD_DIM)
    inputs = tokens.astype(jnp.float32)
    gain_first = gain_attn.astype(jnp.float32)
    gain_second = gain_mlp.astype(jnp.float32)
    normed, recip_attn = norm_forward(inputs, gain_first)
    normed_low = normed.astype(jnp.bfloat16)

    def project(weight):
        return jnp.dot(normed_low, weight, preferred_element_type=jnp.float32).reshape(
            tok_rows, head_count, HEAD_DIM
        )

    queries = rotate(project(w_query), cos_table, sine_table).astype(jnp.bfloat16)
    key_vecs = rotate(project(w_key), cos_table, sine_table).astype(jnp.bfloat16)
    values = project(w_value).astype(jnp.bfloat16)

    def needed(key_first):
        return key_first + tok_rows - 1 >= lowest

    def score_stats(key_block, key_first, maxima, totals):

        def update(stat_pair):
            old_max, old_total = stat_pair
            scores = block_scores(queries, key_block, key_first, query_pos, begins, score_scale)
            new_max = jnp.maximum(old_max, jnp.max(scores, -1))
            new_total = old_total * jnp.exp(old_max - new_max) + jnp.sum(
                jnp.exp(scores - new_max[..., None]), -1
            )
            return (new_max, new_total)

        return lax.cond(needed(key_first), update, lambda stat_pair: stat_pair, (maxima, totals))

    maxima, totals = score_stats(
        key_vecs,
        cycle_place * tok_rows,
        jnp.full((head_count, tok_rows), NEG, jnp.float32),
        jnp.zeros((head_count, tok_rows), jnp.float32),
    )
    stored_keys = lax.dynamic_update_index_in_dim(
        jnp.zeros((back_span + 1,) + key_vecs.shape, jnp.bfloat16), key_vecs, 0, 0
    )
    stored_values = lax.dynamic_update_index_in_dim(
        jnp.zeros((back_span + 1,) + values.shape, jnp.bfloat16), values, 0, 0
    )

    def forward_cycle(step_index, cycle_state):
        key_block, value_block, maxima, totals, stored_keys, stored_values = cycle_state
        key_block, value_block = shifted((key_block, value_block), "ctx", 1)
        maxima, totals = score_stats(
            key_block, (cycle_place - step_index) * tok_rows, maxima, totals
        )
        stored_keys = lax.dynamic_update_index_in_dim(stored_keys, key_block, step_index, 0)
        stored_values = lax.dynamic_update_index_in_dim(stored_values, value_block, step_index, 0)
        return (key_block, value_block, maxima, totals, stored_keys, stored_values)

    cycle_state = lax.fori_loop(
        1,
        back_span + 1,
        forward_cycle,
        (key_vecs, values, maxima, totals, stored_keys, stored_values),
    )
    maxima, totals, stored_keys, stored_values = (
        cycle_state[2],
        cycle_state[3],
        cycle_state[4],
        cycle_state[5],
    )
    log_totals = maxima + jnp.log(totals)

    def output_block(step_index, accum):
        key_block = lax.dynamic_index_in_dim(stored_keys, step_index, 0, keepdims=False)
        value_block = lax.dynamic_index_in_dim(stored_values, step_index, 0, keepdims=False)
        key_first = (cycle_place - step_index) * tok_rows

        def add_block(partials):
            partial_value, remainder_sum = partials
            scores = block_scores(queries, key_block, key_first, query_pos, begins, score_scale)
            weights_full = jnp.exp(scores - log_totals[..., None])
            weights_soft = weights_full.astype(jnp.bfloat16)
            weights_rest = (weights_full - weights_soft.astype(jnp.float32)).astype(jnp.bfloat16)
            partial_value = partial_value + jnp.einsum(
                "hqk,khd->qhd", weights_soft, value_block, preferred_element_type=jnp.float32
            )
            remainder_sum = remainder_sum + jnp.einsum(
                "hqk,khd->qhd", weights_rest, value_block, preferred_element_type=jnp.float32
            )
            return (partial_value, remainder_sum)

        return lax.cond(needed(key_first), add_block, lambda partials: partials, accum)

    attend_zero = jnp.zeros((tok_rows, head_count, HEAD_DIM), jnp.float32)
    attended, remainder_sum = lax.fori_loop(
        0, back_span + 1, output_block, (attend_zero, attend_zero)
    )
    attended_fine = attended + remainder_sum
    attended_low = attended.reshape(tok_rows, model_width).astype(jnp.bfloat16)
    middle = inputs + jnp.dot(attended_low, w_out, preferred_element_type=jnp.float32)
    normed_mlp, recip_mlp = norm_forward(middle, gain_second)
    mlp_low = normed_mlp.astype(jnp.bfloat16)
    gate_pre = jnp.dot(mlp_low, w_gate, preferred_element_type=jnp.float32)
    up_pre = jnp.dot(mlp_low, w_up, preferred_element_type=jnp.float32)
    silu_value = jax.nn.silu(gate_pre)
    hidden_low = (silu_value * up_pre).astype(jnp.bfloat16)
    result = (middle + jnp.dot(hidden_low, w_down, preferred_element_type=jnp.float32)).astype(
        jnp.bfloat16
    )
    grad_w_down = jnp.einsum("tf,td->fd", hidden_low, cotangent, preferred_element_type=jnp.float32)
    grad_hidden = jnp.einsum("td,fd->tf", cotangent, w_down, preferred_element_type=jnp.float32)
    gate_sigmoid = jax.nn.sigmoid(gate_pre)
    grad_gate = (
        grad_hidden * up_pre * gate_sigmoid * (1.0 + gate_pre * (1.0 - gate_sigmoid))
    ).astype(jnp.bfloat16)
    grad_up = (grad_hidden * silu_value).astype(jnp.bfloat16)
    grad_w_gate = jnp.einsum("td,tf->df", mlp_low, grad_gate, preferred_element_type=jnp.float32)
    grad_w_up = jnp.einsum("td,tf->df", mlp_low, grad_up, preferred_element_type=jnp.float32)
    grad_normed_mlp = jnp.einsum(
        "tf,df->td", grad_gate, w_gate, preferred_element_type=jnp.float32
    ) + jnp.einsum("tf,df->td", grad_up, w_up, preferred_element_type=jnp.float32)
    grad_mid_norm, grad_gain_mlp = norm_backward(grad_normed_mlp, middle, recip_mlp, gain_second)
    grad_middle = cotangent.astype(jnp.float32) + grad_mid_norm
    grad_branch = grad_middle.astype(jnp.bfloat16)
    grad_w_out = jnp.einsum(
        "td,te->de", attended_low, grad_branch, preferred_element_type=jnp.float32
    )
    grad_attended = (
        jnp.einsum("te,de->td", grad_branch, w_out, preferred_element_type=jnp.float32)
        .astype(jnp.bfloat16)
        .reshape(tok_rows, head_count, HEAD_DIM)
    )
    row_delta = jnp.einsum("qhd,qhd->hq", grad_attended.astype(jnp.float32), attended_fine)

    def block_grads(key_block, value_block, key_first, grad_queries):
        scores = block_scores(queries, key_block, key_first, query_pos, begins, score_scale)
        probs_full = jnp.exp(scores - log_totals[..., None])
        grad_probs = jnp.einsum(
            "qhd,khd->hqk", grad_attended, value_block, preferred_element_type=jnp.float32
        )
        grad_scores = (probs_full * (grad_probs - row_delta[..., None])).astype(jnp.bfloat16)
        grad_queries = (
            grad_queries
            + jnp.einsum("hqk,khd->qhd", grad_scores, key_block, preferred_element_type=jnp.float32)
            * score_scale
        )
        grad_keys = (
            jnp.einsum("hqk,qhd->khd", grad_scores, queries, preferred_element_type=jnp.float32)
            * score_scale
        )
        grad_values = jnp.einsum(
            "hqk,qhd->khd",
            probs_full.astype(jnp.bfloat16),
            grad_attended,
            preferred_element_type=jnp.float32,
        )
        return (grad_queries, grad_keys, grad_values)

    def block_or_skip(key_block, value_block, key_first, grad_queries):
        empty_grads = jnp.zeros(key_block.shape, jnp.float32)
        return lax.cond(
            needed(key_first),
            lambda inner: block_grads(key_block, value_block, key_first, inner),
            lambda inner: (inner, empty_grads, empty_grads),
            grad_queries,
        )

    query_zero = jnp.zeros((tok_rows, head_count, HEAD_DIM), jnp.float32)
    grad_queries, grad_keys, grad_values = block_or_skip(
        key_vecs, values, cycle_place * tok_rows, query_zero
    )

    def again_step(step_index, again_state):
        key_block, value_block, grad_queries, grad_keys, grad_values = again_state
        key_block, value_block = shifted((key_block, value_block), "ctx", 1)
        grad_keys, grad_values = shifted_2((grad_keys, grad_values), "ctx", 1)
        grad_queries, extra_keys, extra_values = block_or_skip(
            key_block, value_block, (cycle_place - step_index) * tok_rows, grad_queries
        )
        return (
            key_block,
            value_block,
            grad_queries,
            grad_keys + extra_keys,
            grad_values + extra_values,
        )

    again_state = lax.fori_loop(
        1, back_span + 1, again_step, (key_vecs, values, grad_queries, grad_keys, grad_values)
    )
    grad_queries = again_state[2]
    grad_keys, grad_values = (
        shifted_2(again_state[3].astype(jnp.bfloat16), "ctx", -back_span).astype(jnp.float32),
        shifted_2(again_state[4].astype(jnp.bfloat16), "ctx", -back_span).astype(jnp.float32),
    )
    grad_q = (
        rotate_back(grad_queries, cos_table, sine_table)
        .astype(jnp.bfloat16)
        .reshape(tok_rows, model_width)
    )
    grad_k = (
        rotate_back(grad_keys, cos_table, sine_table)
        .astype(jnp.bfloat16)
        .reshape(tok_rows, model_width)
    )
    grad_v = grad_values.astype(jnp.bfloat16).reshape(tok_rows, model_width)
    grad_w_query = jnp.einsum("td,te->de", normed_low, grad_q, preferred_element_type=jnp.float32)
    grad_w_key = jnp.einsum("td,te->de", normed_low, grad_k, preferred_element_type=jnp.float32)
    grad_w_value = jnp.einsum("td,te->de", normed_low, grad_v, preferred_element_type=jnp.float32)
    grad_normed = jnp.einsum("te,de->td", grad_q, w_query, preferred_element_type=jnp.float32)
    grad_normed = grad_normed + jnp.einsum(
        "te,de->td", grad_k, w_key, preferred_element_type=jnp.float32
    )
    grad_normed = grad_normed + jnp.einsum(
        "te,de->td", grad_v, w_value, preferred_element_type=jnp.float32
    )
    grad_in_norm, grad_gain_attn = norm_backward(grad_normed, inputs, recip_attn, gain_first)
    grad_inputs = (grad_middle + grad_in_norm).astype(jnp.bfloat16)
    grads = (
        grad_gain_attn,
        grad_w_query,
        grad_w_key,
        grad_w_value,
        grad_w_out,
        grad_gain_mlp,
        grad_w_gate,
        grad_w_up,
        grad_w_down,
    )
    return (result, grad_inputs, grads)


def body(
    tokens,
    cotangent,
    doc_lengths,
    gain_attn,
    w_query,
    w_key,
    w_value,
    w_out,
    gain_mlp,
    w_gate,
    w_up,
    w_down,
):
    shards = (gain_attn, w_query, w_key, w_value, w_out, gain_mlp, w_gate, w_up, w_down)
    micro_inputs = (tokens[:, 0], cotangent[:, 0], doc_lengths[:, 0])

    def micro_each(grad_totals, micro_item):
        gathered = (
            lax.all_gather(shards[0], "fsdp", axis=0, tiled=True),
            lax.all_gather(shards[1], "fsdp", axis=0, tiled=True),
            lax.all_gather(shards[2], "fsdp", axis=0, tiled=True),
            lax.all_gather(shards[3], "fsdp", axis=0, tiled=True),
            lax.all_gather(shards[4], "fsdp", axis=0, tiled=True),
            lax.all_gather(shards[5], "fsdp", axis=0, tiled=True),
            lax.all_gather(shards[6], "fsdp", axis=0, tiled=True),
            lax.all_gather(shards[7], "fsdp", axis=0, tiled=True),
            lax.all_gather(shards[8], "fsdp", axis=0, tiled=True),
        )
        result, grad_inputs, grads = micro_step(
            gathered, micro_item[0], micro_item[1], micro_item[2]
        )
        part_grads = (
            lax.psum_scatter(
                grads[0].astype(jnp.bfloat16), "fsdp", scatter_dimension=0, tiled=True
            ).astype(jnp.float32),
            lax.psum_scatter(
                grads[1].astype(jnp.bfloat16), "fsdp", scatter_dimension=0, tiled=True
            ).astype(jnp.float32),
            lax.psum_scatter(
                grads[2].astype(jnp.bfloat16), "fsdp", scatter_dimension=0, tiled=True
            ).astype(jnp.float32),
            lax.psum_scatter(
                grads[3].astype(jnp.bfloat16), "fsdp", scatter_dimension=0, tiled=True
            ).astype(jnp.float32),
            lax.psum_scatter(
                grads[4].astype(jnp.bfloat16), "fsdp", scatter_dimension=0, tiled=True
            ).astype(jnp.float32),
            lax.psum_scatter(
                grads[5].astype(jnp.bfloat16), "fsdp", scatter_dimension=0, tiled=True
            ).astype(jnp.float32),
            lax.psum_scatter(
                grads[6].astype(jnp.bfloat16), "fsdp", scatter_dimension=0, tiled=True
            ).astype(jnp.float32),
            lax.psum_scatter(
                grads[7].astype(jnp.bfloat16), "fsdp", scatter_dimension=0, tiled=True
            ).astype(jnp.float32),
            lax.psum_scatter(
                grads[8].astype(jnp.bfloat16), "fsdp", scatter_dimension=0, tiled=True
            ).astype(jnp.float32),
        )
        return (jax.tree.map(jnp.add, grad_totals, part_grads), (result, grad_inputs))

    start_grads = tuple((jnp.zeros(shard.shape, jnp.float32) for shard in shards))
    grad_totals, (results, grad_inputs) = lax.scan(micro_each, start_grads, micro_inputs)
    grad_totals = jax.tree.map(
        lambda part: part.astype(jnp.float32), lax.psum(shortened(grad_totals), "ctx")
    )
    return (
        results[:, None],
        grad_inputs[:, None],
        grad_totals[0],
        grad_totals[1],
        grad_totals[2],
        grad_totals[3],
        grad_totals[4],
        grad_totals[5],
        grad_totals[6],
        grad_totals[7],
        grad_totals[8],
    )


def solution(mesh):
    placed = (
        P(None, "fsdp", "ctx", None),
        P(None, "fsdp", "ctx", None),
        P(None, "fsdp", None),
        P("fsdp"),
        P("fsdp", None),
        P("fsdp", None),
        P("fsdp", None),
        P("fsdp", None),
        P("fsdp"),
        P("fsdp", None),
        P("fsdp", None),
        P("fsdp", None),
    )
    return jax.shard_map(
        body,
        mesh=mesh,
        in_specs=placed,
        out_specs=(
            P(None, "fsdp", "ctx", None),
            P(None, "fsdp", "ctx", None),
            P("fsdp"),
            P("fsdp", None),
            P("fsdp", None),
            P("fsdp", None),
            P("fsdp", None),
            P("fsdp"),
            P("fsdp", None),
            P("fsdp", None),
            P("fsdp", None),
        ),
        check_vma=False,
    )
```

profile of v0, /device:TPU:0, one launch (start us, length us, event | category | flops | bytes accessed | tf_op | source)
XLA Modules:
  0.0 2958.3 jit_solution(17208955619871963077)
XLA Ops:
  12.5 2763.6 %while.210 = (s32[]{:T(128)}, f32[384]{0:T(512)}, f32[384,768]{1,0:T(8,128)}, f32[384,768]{1,0:T(8,128)}, f32[384,768]{1,0:T(8,128)}, /*index=5*/f32[384,768]{1,...) while((s32[]{:T(128)}, f32[384]{0:T(512)}, ...), condition=%wide.region_39.40_spmd.clone, body=%wide.region_0.39_spmd.clone.sunk | while | flops 28005775360 | bytes 898185984 | solution.py:388
  107.2 182.8 %while.211 = (s32[]{:T(128)}, bf16[512,12,64]{0,2,1:T(8,128)(2,1)S(1)}, bf16[512,12,64]{0,2,1:T(8,128)(2,1)}, f32[12,512]{1,0:T(8,128)}, f32[12,512]{1,0:T(8,128...) while((s32[]{:T(128)}, ...), condition=%wide.region_14.14_spmd.clone, body=%wide.region_9.13_spmd.clone.sunk | while | flops 425473024 | bytes 40442304 | solution.py:150
  367.5 651.2 %while.213 = (s32[]{:T(128)}, bf16[512,12,64]{0,2,1:T(8,128)(2,1)S(1)}, bf16[512,12,64]{0,2,1:T(8,128)(2,1)}, f32[512,12,64]{0,2,1:T(8,128)}, f32[512,12,64]{0,2...) while((s32[]{:T(128)}, ...), condition=%wide.region_26.26_spmd.clone, body=%wide.region_23.25_spmd.clone.sunk | while | flops 2047476736 | bytes 119626376 | solution.py:279
  461.1 28.8 collective-permute-start.4
  497.6 27.9 collective-permute-start.2
  587.0 31.6 %collective-permute-start.2 = (bf16[512,12,64]{0,2,1:T(8,128)(2,1)S(1)}, bf16[512,12,64]{0,2,1:T(8,128)(2,1)S(1)}, u32[]{:S(2)}, u32[]{:S(2)}) collective-permute-start(bf16[512,12,64]{0,2,1:T(8,128)(2,1)S(1)} %get-tuple-element.3526), channel_id=1, source_target_pairs={{0,2},{2,4},{4,6},{6,8},{8,10},{10,12},{12,14},{14,16},{16,18},{18... | collective-permute-start | bytes 2359304 | tf_op jit(solution)/shard_map/while/body/eval_jaxpr/while/body/eval_jaxpr/ppermute | solution.py:17
  663.2 36.4 %collective-permute-start.2 = (bf16[512,12,64]{0,2,1:T(8,128)(2,1)S(1)}, bf16[512,12,64]{0,2,1:T(8,128)(2,1)S(1)}, u32[]{:S(2)}, u32[]{:S(2)}) collective-permute-start(bf16[512,12,64]{0,2,1:T(8,128)(2,1)S(1)} %get-tuple-element.3526), channel_id=1, source_target_pairs={{0,2},{2,4},{4,6},{6,8},{8,10},{10,12},{12,14},{14,16},{16,18},{18... | collective-permute-start | bytes 2359304 | tf_op jit(solution)/shard_map/while/body/eval_jaxpr/while/body/eval_jaxpr/ppermute | solution.py:17
  860.6 39.4 %collective-permute-start.4 = (f32[512,12,64]{0,2,1:T(8,128)}, f32[512,12,64]{0,2,1:T(8,128)}, u32[]{:S(2)}, u32[]{:S(2)}) collective-permute-start(f32[512,12,64]{0,2,1:T(8,128)} %get-tuple-element.3529), channel_id=1, source_target_pairs={{0,2},{2,4},{4,6},{6,8},{8,10},{10,12},{12,14},{14,16},{16,18},{18... | collective-permute-start | bytes 4718600 | tf_op jit(solution)/shard_map/while/body/eval_jaxpr/while/body/eval_jaxpr/ppermute | solution.py:22
  1020.2 167.8 %collective-permute-start.7 = (bf16[512,12,64]{0,2,1:T(8,128)(2,1)S(1)}, bf16[512,12,64]{0,2,1:T(8,128)(2,1)S(1)}, u32[]{:S(2)}, u32[]{:S(2)}) collective-permute-start(bf16[512,12,64]{0,2,1:T(8,128)(2,1)S(1)} %convert_element_type.990), channel_id=1, source_target_pairs={{0,16},{2,18},{4,20},{6,22},{8,24},{10,26},{12,28},{14,30},{16,0},... | collective-permute-start | bytes 2359304 | tf_op jit(solution)/shard_map/while/body/eval_jaxpr/ppermute | solution.py:22
  1276.5 44.1 %reduce-scatter.18.cloned.1.call-done = bf16[384,2048]{1,0:T(8,128)(2,1)} async-done(((bf16[768,2048]{1,0:T(8,128)(2,1)}), bf16[384,2048]{1,0:T(8,128)(2,1)}) %reduce-scatter.18.cloned.1.call-update) | async-done | bytes 1572880 | tf_op jit(solution)/shard_map/while/body/eval_jaxpr/reduce_scatter | solution.py:378
  1324.5 41.8 %reduce-scatter.16.cloned.1.call-done = bf16[384,2048]{1,0:T(8,128)(2,1)} async-done(((bf16[768,2048]{1,0:T(8,128)(2,1)}), bf16[384,2048]{1,0:T(8,128)(2,1)}) %reduce-scatter.16.cloned.1.call-update) | async-done | bytes 1572880 | tf_op jit(solution)/shard_map/while/body/eval_jaxpr/reduce_scatter | solution.py:375
  1368.7 43.1 %reduce-scatter.20.cloned.1.call-done = bf16[1024,768]{1,0:T(8,128)(2,1)} async-done(((bf16[2048,768]{1,0:T(8,128)(2,1)}), bf16[1024,768]{1,0:T(8,128)(2,1)}) %reduce-scatter.20.cloned.1.call-update) | async-done | bytes 1572880 | tf_op jit(solution)/shard_map/while/body/eval_jaxpr/reduce_scatter | solution.py:381
  1506.4 182.8 %while.211 = (s32[]{:T(128)}, bf16[512,12,64]{0,2,1:T(8,128)(2,1)S(1)}, bf16[512,12,64]{0,2,1:T(8,128)(2,1)}, f32[12,512]{1,0:T(8,128)}, f32[12,512]{1,0:T(8,128...) while((s32[]{:T(128)}, ...), condition=%wide.region_14.14_spmd.clone, body=%wide.region_9.13_spmd.clone.sunk | while | flops 425473024 | bytes 40442304 | solution.py:150
  1766.8 598.9 %while.213 = (s32[]{:T(128)}, bf16[512,12,64]{0,2,1:T(8,128)(2,1)S(1)}, bf16[512,12,64]{0,2,1:T(8,128)(2,1)}, f32[512,12,64]{0,2,1:T(8,128)}, f32[512,12,64]{0,2...) while((s32[]{:T(128)}, ...), condition=%wide.region_26.26_spmd.clone, body=%wide.region_23.25_spmd.clone.sunk | while | flops 2047476736 | bytes 119626376 | solution.py:279
  1821.2 51.2 %collective-permute-start.4 = (f32[512,12,64]{0,2,1:T(8,128)}, f32[512,12,64]{0,2,1:T(8,128)}, u32[]{:S(2)}, u32[]{:S(2)}) collective-permute-start(f32[512,12,64]{0,2,1:T(8,128)} %get-tuple-element.3529), channel_id=1, source_target_pairs={{0,2},{2,4},{4,6},{6,8},{8,10},{10,12},{12,14},{14,16},{16,18},{18... | collective-permute-start | bytes 4718600 | tf_op jit(solution)/shard_map/while/body/eval_jaxpr/while/body/eval_jaxpr/ppermute | solution.py:22
  1907.8 28.0 collective-permute-start.4
  1981.1 40.7 %collective-permute-start.4 = (f32[512,12,64]{0,2,1:T(8,128)}, f32[512,12,64]{0,2,1:T(8,128)}, u32[]{:S(2)}, u32[]{:S(2)}) collective-permute-start(f32[512,12,64]{0,2,1:T(8,128)} %get-tuple-element.3529), channel_id=1, source_target_pairs={{0,2},{2,4},{4,6},{6,8},{8,10},{10,12},{12,14},{14,16},{16,18},{18... | collective-permute-start | bytes 4718600 | tf_op jit(solution)/shard_map/while/body/eval_jaxpr/while/body/eval_jaxpr/ppermute | solution.py:22
  2169.7 35.1 %collective-permute-start.2 = (bf16[512,12,64]{0,2,1:T(8,128)(2,1)S(1)}, bf16[512,12,64]{0,2,1:T(8,128)(2,1)S(1)}, u32[]{:S(2)}, u32[]{:S(2)}) collective-permute-start(bf16[512,12,64]{0,2,1:T(8,128)(2,1)S(1)} %get-tuple-element.3526), channel_id=1, source_target_pairs={{0,2},{2,4},{4,6},{6,8},{8,10},{10,12},{12,14},{14,16},{16,18},{18... | collective-permute-start | bytes 2359304 | tf_op jit(solution)/shard_map/while/body/eval_jaxpr/while/body/eval_jaxpr/ppermute | solution.py:17
  2367.2 99.9 %collective-permute-start.7 = (bf16[512,12,64]{0,2,1:T(8,128)(2,1)S(1)}, bf16[512,12,64]{0,2,1:T(8,128)(2,1)S(1)}, u32[]{:S(2)}, u32[]{:S(2)}) collective-permute-start(bf16[512,12,64]{0,2,1:T(8,128)(2,1)S(1)} %convert_element_type.990), channel_id=1, source_target_pairs={{0,16},{2,18},{4,20},{6,22},{8,24},{10,26},{12,28},{14,30},{16,0},... | collective-permute-start | bytes 2359304 | tf_op jit(solution)/shard_map/while/body/eval_jaxpr/ppermute | solution.py:22
  2633.8 44.1 %reduce-scatter.18.cloned.1.call-done = bf16[384,2048]{1,0:T(8,128)(2,1)} async-done(((bf16[768,2048]{1,0:T(8,128)(2,1)}), bf16[384,2048]{1,0:T(8,128)(2,1)}) %reduce-scatter.18.cloned.1.call-update) | async-done | bytes 1572880 | tf_op jit(solution)/shard_map/while/body/eval_jaxpr/reduce_scatter | solution.py:378
  2682.8 40.7 %reduce-scatter.16.cloned.1.call-done = bf16[384,2048]{1,0:T(8,128)(2,1)} async-done(((bf16[768,2048]{1,0:T(8,128)(2,1)}), bf16[384,2048]{1,0:T(8,128)(2,1)}) %reduce-scatter.16.cloned.1.call-update) | async-done | bytes 1572880 | tf_op jit(solution)/shard_map/while/body/eval_jaxpr/reduce_scatter | solution.py:375
  2726.0 43.3 %reduce-scatter.20.cloned.1.call-done = bf16[1024,768]{1,0:T(8,128)(2,1)} async-done(((bf16[2048,768]{1,0:T(8,128)(2,1)}), bf16[1024,768]{1,0:T(8,128)(2,1)}) %reduce-scatter.20.cloned.1.call-update) | async-done | bytes 1572880 | tf_op jit(solution)/shard_map/while/body/eval_jaxpr/reduce_scatter | solution.py:381
  2788.0 34.6 %all-reduce.5 = (bf16[384]{0:T(512)(128)(2,1)S(1)}, bf16[384]{0:T(512)(128)(2,1)S(1)}) all-reduce(bf16[384]{0:T(512)(128)(2,1)S(1)} %convert_element_type.672, bf16[384]{0:T(512)(128)(2,1)S(1)} %convert_element_type.682), channel_id=1, replica_groups=mesh['ctx'=16,'fsdp'=2] {'ctx'}, use_global_device_ids=true, to_apply=%region_40.41 | all-reduce | flops 768 | bytes 3072 | tf_op jit(solution)/shard_map/psum | solution.py:390
  2823.8 114.7 %all-reduce.11.cloned.1.call-done = (bf16[384,768]{1,0:T(8,128)(2,1)}, bf16[384,768]{1,0:T(8,128)(2,1)}, bf16[384,768]{1,0:T(8,128)(2,1)}, bf16[384,768]{1,0:T(8...) async-done(((bf16[384,768]{1,0:T(8,128)(2,1)}, bf16[384,768]{1,0:T(8,128)(2,1)}, bf16[384,768]{1,0:T(8,128)(2,1)}, ...) | async-done | bytes 7077904 | tf_op jit(solution)/shard_map/psum | solution.py:390
  (1181 shorter events, 2022.2 us)
Async XLA Ops:
  15.0 297.1 %all-gather.22.cloned.1.call-start = ((), (), s32[]{:S(2)}) async-start(), calls=%async_computation.11 | async-start | bytes 1769472 | tf_op jit(solution)/shard_map/while/body/eval_jaxpr/all_gather | solution.py:347
  15.6 301.7 %all-gather.26.cloned.1.call-start = ((), (), s32[]{:S(2)}) async-start(), calls=%async_computation.13 | async-start | bytes 4718592 | tf_op jit(solution)/shard_map/while/body/eval_jaxpr/all_gather | solution.py:351
  16.1 307.1 %all-gather.24.cloned.1.call-start = ((), (), s32[]{:S(2)}) async-start(), calls=%async_computation.12 | async-start | bytes 4718592 | tf_op jit(solution)/shard_map/while/body/eval_jaxpr/all_gather | solution.py:349
  16.7 312.3 %all-gather.28.cloned.1.call-start = ((), (), s32[]{:S(2)}) async-start(), calls=%async_computation.14 | async-start | bytes 4718592 | tf_op jit(solution)/shard_map/while/body/eval_jaxpr/all_gather | solution.py:350
  17.5 1246.7 %reduce-scatter.14.cloned.1.call-start = ((), (), s32[]{:S(2)}) async-start(), calls=%async_computation.18 | async-start | bytes 1769472 | tf_op jit(solution)/shard_map/while/body/eval_jaxpr/reduce_scatter | solution.py:369
  347.7 918.8 %reduce-scatter.8.cloned.1.call-start = ((), (), s32[]{:S(2)}) async-start(), calls=%async_computation.15 | async-start | bytes 1769472 | tf_op jit(solution)/shard_map/while/body/eval_jaxpr/reduce_scatter | solution.py:360
  367.5 87.5 %collective-permute-start.4 = (f32[512,12,64]{0,2,1:T(8,128)}, f32[512,12,64]{0,2,1:T(8,128)}, u32[]{:S(2)}, u32[]{:S(2)}) collective-permute-start(f32[512,12,64]{0,2,1:T(8,128)} %get-tuple-element.3529), channel_id=1, source_target_pairs={{0,2},{2,4},{4,6},{6,8},{8,10},{10,12},{12,14},{14,16},{16,18},{18... | collective-permute-start | bytes 4718600 | tf_op jit(solution)/shard_map/while/body/eval_jaxpr/while/body/eval_jaxpr/ppermute | solution.py:22
  1020.2 177.7 %collective-permute-start.7 = (bf16[512,12,64]{0,2,1:T(8,128)(2,1)S(1)}, bf16[512,12,64]{0,2,1:T(8,128)(2,1)S(1)}, u32[]{:S(2)}, u32[]{:S(2)}) collective-permute-start(bf16[512,12,64]{0,2,1:T(8,128)(2,1)S(1)} %convert_element_type.990), channel_id=1, source_target_pairs={{0,16},{2,18},{4,20},{6,22},{8,24},{10,26},{12,28},{14,30},{16,0},... | collective-permute-start | bytes 2359304 | tf_op jit(solution)/shard_map/while/body/eval_jaxpr/ppermute | solution.py:22
  1227.0 93.6 %reduce-scatter.18.cloned.1.call-start = ((), (), s32[]{:S(2)}) async-start(), calls=%async_computation.20 | async-start | bytes 4718592 | tf_op jit(solution)/shard_map/while/body/eval_jaxpr/reduce_scatter | solution.py:378
  1232.2 134.1 %reduce-scatter.16.cloned.1.call-start = ((), (), s32[]{:S(2)}) async-start(), calls=%async_computation.19 | async-start | bytes 4718592 | tf_op jit(solution)/shard_map/while/body/eval_jaxpr/reduce_scatter | solution.py:375
  1237.3 174.5 %reduce-scatter.20.cloned.1.call-start = ((), (), s32[]{:S(2)}) async-start(), calls=%async_computation.21 | async-start | bytes 4718592 | tf_op jit(solution)/shard_map/while/body/eval_jaxpr/reduce_scatter | solution.py:381
  1417.5 294.0 %all-gather.22.cloned.1.call-start = ((), (), s32[]{:S(2)}) async-start(), calls=%async_computation.11 | async-start | bytes 1769472 | tf_op jit(solution)/shard_map/while/body/eval_jaxpr/all_gather | solution.py:347
  1418.1 298.6 %all-gather.26.cloned.1.call-start = ((), (), s32[]{:S(2)}) async-start(), calls=%async_computation.13 | async-start | bytes 4718592 | tf_op jit(solution)/shard_map/while/body/eval_jaxpr/all_gather | solution.py:351
  1418.8 304.0 %all-gather.24.cloned.1.call-start = ((), (), s32[]{:S(2)}) async-start(), calls=%async_computation.12 | async-start | bytes 4718592 | tf_op jit(solution)/shard_map/while/body/eval_jaxpr/all_gather | solution.py:349
  1419.4 309.1 %all-gather.28.cloned.1.call-start = ((), (), s32[]{:S(2)}) async-start(), calls=%async_computation.14 | async-start | bytes 4718592 | tf_op jit(solution)/shard_map/while/body/eval_jaxpr/all_gather | solution.py:350
  1420.1 1134.0 %reduce-scatter.14.cloned.1.call-start = ((), (), s32[]{:S(2)}) async-start(), calls=%async_computation.18 | async-start | bytes 1769472 | tf_op jit(solution)/shard_map/while/body/eval_jaxpr/reduce_scatter | solution.py:369
  1747.2 837.2 %reduce-scatter.8.cloned.1.call-start = ((), (), s32[]{:S(2)}) async-start(), calls=%async_computation.15 | async-start | bytes 1769472 | tf_op jit(solution)/shard_map/while/body/eval_jaxpr/reduce_scatter | solution.py:360
  2367.2 118.3 %collective-permute-start.7 = (bf16[512,12,64]{0,2,1:T(8,128)(2,1)S(1)}, bf16[512,12,64]{0,2,1:T(8,128)(2,1)S(1)}, u32[]{:S(2)}, u32[]{:S(2)}) collective-permute-start(bf16[512,12,64]{0,2,1:T(8,128)(2,1)S(1)} %convert_element_type.990), channel_id=1, source_target_pairs={{0,16},{2,18},{4,20},{6,22},{8,24},{10,26},{12,28},{14,30},{16,0},... | collective-permute-start | bytes 2359304 | tf_op jit(solution)/shard_map/while/body/eval_jaxpr/ppermute | solution.py:22
  2493.8 114.5 %reduce-scatter.10.cloned.1.call-start = ((), (), s32[]{:S(2)}) async-start(), calls=%async_computation.16 | async-start | bytes 1769472 | tf_op jit(solution)/shard_map/while/body/eval_jaxpr/reduce_scatter | solution.py:363
  2497.3 135.1 %reduce-scatter.12.cloned.1.call-start = ((), (), s32[]{:S(2)}) async-start(), calls=%async_computation.17 | async-start | bytes 1769472 | tf_op jit(solution)/shard_map/while/body/eval_jaxpr/reduce_scatter | solution.py:366
  2516.8 161.2 %reduce-scatter.18.cloned.1.call-start = ((), (), s32[]{:S(2)}) async-start(), calls=%async_computation.20 | async-start | bytes 4718592 | tf_op jit(solution)/shard_map/while/body/eval_jaxpr/reduce_scatter | solution.py:378
  2522.0 201.6 %reduce-scatter.16.cloned.1.call-start = ((), (), s32[]{:S(2)}) async-start(), calls=%async_computation.19 | async-start | bytes 4718592 | tf_op jit(solution)/shard_map/while/body/eval_jaxpr/reduce_scatter | solution.py:375
  2527.2 242.1 %reduce-scatter.20.cloned.1.call-start = ((), (), s32[]{:S(2)}) async-start(), calls=%async_computation.21 | async-start | bytes 4718592 | tf_op jit(solution)/shard_map/while/body/eval_jaxpr/reduce_scatter | solution.py:381
  2776.1 162.5 %all-reduce.11.cloned.1.call-start = ((), (), s32[]{:S(2)}) async-start(), calls=%async_computation.7 | async-start | bytes 14155776 | tf_op jit(solution)/shard_map/psum | solution.py:390
  (318 other events, 5898.5 us)
Sparse Core Ops, SparseCore 0:
  15.1 25.4 all-gather.15
  42.2 22.7 all-gather.17
  66.5 22.7 all-gather.19
  90.7 22.7 all-gather.21
  114.9 44.8 all-gather.25
  161.2 44.8 all-gather.23
  207.7 44.8 all-gather.27
  347.8 148.2 reduce-scatter.13
  1253.1 21.8 reduce-scatter.11
  1277.2 43.3 reduce-scatter.17
  1322.8 43.4 reduce-scatter.15
  1368.4 43.4 reduce-scatter.19
  1417.8 22.8 all-gather.15
  1442.0 22.7 all-gather.17
  1466.2 22.7 all-gather.19
  1490.4 22.7 all-gather.21
  1514.7 44.8 all-gather.25
  1561.1 44.8 all-gather.23
  1607.6 44.8 all-gather.27
  1747.3 147.1 reduce-scatter.13
  2493.9 90.4 reduce-scatter.7
  2634.5 43.4 reduce-scatter.17
  2680.1 43.4 reduce-scatter.15
  2725.8 43.4 reduce-scatter.19
  (4 shorter events, 85.7 us)
Sparse Core Ops, SparseCore 1:
  2787.4 151.0 all-reduce.10
where the time goes:
time: 2960 us
  starting transfers between devices  1620 us (55%)
  waiting for transfers between devices  653 us (22%)
  matrix products  204 us (7%)
  other arithmetic  202 us (7%)
  local copies, waits for them, and re-layouts  155 us (5%)
  blocking collectives  63.8 us (2%)
  loops' own time  44.1 us (1%)
    ppermute x36, starting transfers between devices, shifted_2(): lax.ppermute(shard, axis, [(i, (i + by) % size) for i in range(size)])  824 us
    ppermute x64, starting transfers between devices, shifted(): lax.ppermute(value, axis, [(source, source + steps) for source in range(i...  794 us
    psum x1, waiting for transfers between devices, body(): lax.psum(shortened(grad_totals), 'ctx')  115 us
    while x454, local copies, waits for them, and re-layouts  92.3 us
    reduce_scatter x2, waiting for transfers between devices, micro_each(): lax.psum_scatter(grads[7].astype(jnp.bfloat16), 'fsdp', scatter_dimension...  88.2 us
    reduce_scatter x2, waiting for transfers between devices, micro_each(): lax.psum_scatter(grads[8].astype(jnp.bfloat16), 'fsdp', scatter_dimension...  86.4 us
    reduce_scatter x2, waiting for transfers between devices, micro_each(): lax.psum_scatter(grads[6].astype(jnp.bfloat16), 'fsdp', scatter_dimension...  82.5 us
  transfers between devices with their start and end apart: 129, of which 54 were waited for; matrix products, arithmetic and copies ran while one was open for 15% of the time, Pallas kernels for 0%

commit v1 on v0

v1 whole, which is shorter than its diff:
```python
import functools
import math

import jax
import jax.numpy as jnp
from jax import lax
from jax.experimental import pallas as pl
from jax.experimental.pallas import tpu as pltpu
from jax.sharding import PartitionSpec as P

HEAD_DIM = 64
LANES = 128
EPS = 1e-05
NEG = -1e30
LOG2E = math.log2(math.e)
LN2 = math.log(2.0)
F32 = jnp.float32
BF16 = jnp.bfloat16


def dot_nt(left, right):
    return lax.dot_general(left, right, (((1,), (1,)), ((), ())), preferred_element_type=F32)


def dot_nn(left, right):
    return lax.dot_general(left, right, (((1,), (0,)), ((), ())), preferred_element_type=F32)


def dot_tn(left, right):
    return lax.dot_general(left, right, (((0,), (0,)), ((), ())), preferred_element_type=F32)


def lane_index(rows):
    return lax.broadcasted_iota(jnp.int32, (rows, LANES), 1)


def flip(tile):
    return pltpu.roll(tile, HEAD_DIM, 1)


def params(count):
    return pltpu.CompilerParams(
        dimension_semantics=("arbitrary",) * count, vmem_limit_bytes=60 * 1024 * 1024
    )


def full_block(shape):
    zeros = (0,) * len(shape)
    return pl.BlockSpec(shape, lambda *_: zeros)


def pack_pair(tile):
    count = tile.shape[0] // 2
    low = lane_index(count) < HEAD_DIM
    top, bottom = tile[:count], tile[count:]
    return (jnp.where(low, top, flip(bottom)), jnp.where(low, flip(top), bottom))


def unpack_pair(first, second):
    low = lane_index(first.shape[0]) < HEAD_DIM
    top = jnp.where(low, first, flip(second))
    bottom = jnp.where(low, flip(first), second)
    return jnp.concatenate([top, bottom], 0)


def turn(tile):
    near = (lane_index(tile.shape[0]) % HEAD_DIM) < HEAD_DIM // 2
    return jnp.where(
        near, pltpu.roll(tile, LANES - HEAD_DIM // 2, 1), pltpu.roll(tile, HEAD_DIM // 2, 1)
    )


def project_kernel(pieces, x_ref, g_ref, c_ref, s_ref, wq_ref, wk_ref, wv_ref, n_ref, *outs):
    x = x_ref[...].astype(F32)
    recip = lax.rsqrt(jnp.mean(x * x, -1, keepdims=True) + EPS)
    normed = (x * recip * g_ref[...].astype(F32)).astype(BF16)
    n_ref[...] = normed
    queries = dot_nn(normed, wq_ref[...])
    key_vecs = dot_nn(normed, wk_ref[...])
    values = dot_nn(normed, wv_ref[...])
    cos_table, sine_table = c_ref[...], s_ref[...]
    rows = x.shape[0]
    low = lane_index(rows) < HEAD_DIM
    place = {}
    for out_index, (first, count) in enumerate(pieces):
        for unit in range(first, first + count):
            place[unit] = (out_index, unit - first)
    for pair in range(x.shape[1] // LANES):
        cut = slice(pair * LANES, (pair + 1) * LANES)
        q2, k2, v2 = queries[:, cut], key_vecs[:, cut], values[:, cut]
        q2 = (q2 * cos_table + turn(q2) * sine_table) * (LOG2E * HEAD_DIM**-0.5)
        k2 = k2 * cos_table + turn(k2) * sine_table
        packed = pack_pair(q2)
        kv = (jnp.where(low, k2, flip(v2)), jnp.where(low, flip(k2), v2))
        for side in range(2):
            out_index, spot = place[2 * pair + side]
            outs[out_index][spot, 0, :rows, :] = kv[side].astype(BF16)
            outs[out_index][spot, 0, rows:, :] = packed[side].astype(BF16)


def project(pieces, tokens, gain, cos_table, sine_table, w_query, w_key, w_value):
    rows, width = tokens.shape
    half = rows // 2
    depth = half + half // 2
    return pl.pallas_call(
        functools.partial(project_kernel, pieces),
        grid=(2,),
        in_specs=[
            pl.BlockSpec((half, width), lambda i: (i, 0)),
            full_block((1, width)),
            pl.BlockSpec((half, LANES), lambda i: (i, 0)),
            pl.BlockSpec((half, LANES), lambda i: (i, 0)),
            full_block((width, width)),
            full_block((width, width)),
            full_block((width, width)),
        ],
        out_specs=[pl.BlockSpec((half, width), lambda i: (i, 0))]
        + [pl.BlockSpec((count, 1, depth, LANES), lambda i: (0, i, 0, 0)) for _, count in pieces],
        out_shape=[jax.ShapeDtypeStruct((rows, width), BF16)]
        + [jax.ShapeDtypeStruct((count, 2, depth, LANES), BF16) for _, count in pieces],
        compiler_params=params(1),
        cost_estimate=pl.CostEstimate(
            flops=6 * rows * width * width, bytes_accessed=12 * width * width, transcendentals=0
        ),
        name="project",
    )(tokens, gain, cos_table, sine_table, w_query, w_key, w_value)


def row_begins(starts_ref, positions):
    begins = jnp.zeros_like(positions)
    for index in range(starts_ref.shape[0]):
        start = starts_ref[index]
        begins = jnp.maximum(begins, jnp.where(positions >= start, start, 0))
    return begins


def unpack_one(packed, lanes_low):
    wide = packed.astype(F32)
    low = lane_index(wide.shape[0]) < HEAD_DIM
    keep = low if lanes_low else jnp.logical_not(low)
    turned = flip(wide)
    first, second = (wide, turned) if lanes_low else (turned, wide)
    return jnp.concatenate(
        [jnp.where(keep, first, 0.0), jnp.where(keep, second, 0.0)], 0
    ).astype(BF16)


def attend_kernel(info, starts, mine, other, o_ref, lse_ref):
    block = pl.program_id(0)
    core = info[0]
    lowest, inner = info[1 + 2 * block], info[2 + 2 * block]
    rows = mine.shape[1] * 2 // 3
    low = lane_index(rows) < HEAD_DIM
    queries = unpack_one(mine[block, rows:, :], True)
    row_pos = (2 * block + core) * rows + lax.broadcasted_iota(jnp.int32, (rows, 1), 0)
    begins = row_begins(starts, row_pos)
    lane_low = lane_index(2 * rows) < HEAD_DIM
    column = lax.broadcasted_iota(jnp.int32, (1, 2 * rows), 1)
    offsets = jnp.where(column < rows, column + core * rows, column - core * rows)

    def step(masked, index, carry):
        peak, acc = carry
        kv = jnp.concatenate([mine[index, :rows, :], other[index, :rows, :]], 0)
        ones_v = jnp.where(lane_low, jnp.ones_like(kv), kv)
        scores = dot_nt(queries, kv)
        if masked:
            key_pos = offsets + index * (2 * rows)
            scores = jnp.where((key_pos >= begins) & (key_pos <= row_pos), scores, NEG)
        new_peak = jnp.maximum(peak, jnp.max(scores, -1, keepdims=True))
        weights = jnp.exp2(scores - new_peak)
        acc = acc * jnp.exp2(peak - new_peak) + dot_nn(weights.astype(BF16), ones_v)
        return (new_peak, acc)

    carry = step(True, block, (jnp.full((rows, 1), NEG, F32), jnp.zeros((rows, LANES), F32)))
    carry = lax.fori_loop(lowest, inner, functools.partial(step, True), carry)
    peak, acc = lax.fori_loop(inner, block, functools.partial(step, False), carry)
    result = acc / flip(acc)
    count = rows // 2
    small_low = lane_index(count) < HEAD_DIM
    o_ref[0] = jnp.where(small_low, flip(result[:count]), result[count:]).astype(BF16)
    lse = jnp.where(low, peak + jnp.log2(acc), 0.0)
    lse_ref[0] = jnp.transpose(lse)[0:1, :]


def attend(info, starts, mine, other):
    blocks, depth, _ = mine.shape
    rows = depth * 2 // 3
    return pl.pallas_call(
        attend_kernel,
        grid_spec=pltpu.PrefetchScalarGridSpec(
            num_scalar_prefetch=2,
            grid=(blocks,),
            in_specs=[
                pl.BlockSpec(mine.shape, lambda i, *_: (0, 0, 0)),
                pl.BlockSpec(other.shape, lambda i, *_: (0, 0, 0)),
            ],
            out_specs=[
                pl.BlockSpec((1, rows // 2, LANES), lambda i, *_: (i, 0, 0)),
                pl.BlockSpec((1, 1, rows), lambda i, *_: (i, 0, 0)),
            ],
        ),
        out_shape=[
            jax.ShapeDtypeStruct((blocks, rows // 2, LANES), BF16),
            jax.ShapeDtypeStruct((blocks, 1, rows), F32),
        ],
        compiler_params=params(1),
        cost_estimate=pl.CostEstimate(
            flops=16 * 10**9, bytes_accessed=10**7, transcendentals=10**7
        ),
        name="attend",
    )(info, starts, mine, other)


def attend_grad_kernel(
    info, starts, mine, other, do_ref, o_ref, lse_ref, dm_ref, dp_ref, acc_mine, acc_other
):
    block = pl.program_id(0)
    core = info[0]
    lowest, inner = info[1 + 2 * block], info[2 + 2 * block]
    rows = mine.shape[1] * 2 // 3
    count = rows // 2

    @pl.when(block == 0)
    def _():
        acc_mine[...] = jnp.zeros_like(acc_mine)
        acc_other[...] = jnp.zeros_like(acc_other)

    queries = unpack_one(mine[block, rows:, :], True)
    grad_out = unpack_one(do_ref[0], False)
    both = jnp.concatenate([queries, grad_out], 0)
    product = jnp.transpose(do_ref[0].astype(F32) * o_ref[0].astype(F32))
    delta = jnp.concatenate(
        [
            jnp.sum(product[:HEAD_DIM], 0, keepdims=True),
            jnp.sum(product[HEAD_DIM:], 0, keepdims=True),
        ],
        1,
    )
    lse = lse_ref[0]
    row_pos = (2 * block + core) * rows + lax.broadcasted_iota(jnp.int32, (1, rows), 1)
    begins = row_begins(starts, row_pos)
    line = lax.broadcasted_iota(jnp.int32, (2 * rows, 1), 0)
    offsets = jnp.where(line < rows, line + core * rows, line - core * rows)

    def step(masked, index, grad_q):
        kv = jnp.concatenate([mine[index, :rows, :], other[index, :rows, :]], 0)
        scores = dot_nt(kv, queries)
        weights = jnp.exp2(scores - lse)
        if masked:
            key_pos = offsets + index * (2 * rows)
            weights = jnp.where((key_pos >= begins) & (key_pos <= row_pos), weights, 0.0)
        grad_weights = dot_nt(kv, grad_out)
        grad_scores = (weights * (grad_weights - delta)).astype(BF16)
        grad_kv = dot_nn(jnp.concatenate([grad_scores, weights.astype(BF16)], 1), both)
        acc_mine[index] += grad_kv[:rows]
        acc_other[index] += grad_kv[rows:]
        return grad_q + dot_tn(grad_scores, kv)

    grad_q = step(True, block, jnp.zeros((rows, LANES), F32))
    grad_q = lax.fori_loop(lowest, inner, functools.partial(step, True), grad_q)
    grad_q = lax.fori_loop(inner, block, functools.partial(step, False), grad_q)
    grad_q = grad_q * HEAD_DIM**-0.5
    small_low = lane_index(count) < HEAD_DIM
    dm_ref[block, rows:, :] = jnp.where(small_low, grad_q[:count], flip(grad_q[count:])).astype(
        BF16
    )

    @pl.when(block == pl.num_programs(0) - 1)
    def _():
        scale = jnp.where(lane_index(rows) < HEAD_DIM, LN2, 1.0)

        def flush(index, _):
            dm_ref[index, :rows, :] = (acc_mine[index] * scale).astype(BF16)
            dp_ref[index] = (acc_other[index] * scale).astype(BF16)
            return 0

        lax.fori_loop(0, mine.shape[0], flush, 0)


def attend_grad(info, starts, mine, other, grad_out, out, lse):
    blocks, depth, _ = mine.shape
    rows = depth * 2 // 3
    whole = pl.BlockSpec(mine.shape, lambda i, *_: (0, 0, 0))
    small = pl.BlockSpec((1, rows // 2, LANES), lambda i, *_: (i, 0, 0))
    return pl.pallas_call(
        attend_grad_kernel,
        grid_spec=pltpu.PrefetchScalarGridSpec(
            num_scalar_prefetch=2,
            grid=(blocks,),
            in_specs=[
                whole,
                whole,
                small,
                small,
                pl.BlockSpec((1, 1, rows), lambda i, *_: (i, 0, 0)),
            ],
            out_specs=[whole, pl.BlockSpec((blocks, rows, LANES), lambda i, *_: (0, 0, 0))],
            scratch_shapes=[
                pltpu.VMEM((blocks, rows, LANES), F32),
                pltpu.VMEM((blocks, rows, LANES), F32),
            ],
        ),
        out_shape=[
            jax.ShapeDtypeStruct(mine.shape, BF16),
            jax.ShapeDtypeStruct((blocks, rows, LANES), BF16),
        ],
        compiler_params=params(1),
        cost_estimate=pl.CostEstimate(
            flops=32 * 10**9, bytes_accessed=10**7, transcendentals=10**7
        ),
        name="attend_grad",
    )(info, starts, mine, other, grad_out, out, lse)


def collect_kernel(spots, *refs):
    ins, out = refs[:-1], refs[-1]
    for pair in range(len(spots) // 2):
        tiles = []
        for side in range(2):
            array, spot = spots[2 * pair + side]
            tiles.append(ins[array][spot, 0].astype(F32))
        out[:, pair * LANES : (pair + 1) * LANES] = unpack_pair(*tiles).astype(BF16)


def collect(spots, arrays):
    units, _, count, _ = arrays[0].shape
    width = len(spots) * HEAD_DIM
    return pl.pallas_call(
        functools.partial(collect_kernel, spots),
        grid=(2,),
        in_specs=[
            pl.BlockSpec((units, 1, count, LANES), lambda i: (0, i, 0, 0)) for _ in arrays
        ],
        out_specs=pl.BlockSpec((2 * count, width), lambda i: (i, 0)),
        out_shape=jax.ShapeDtypeStruct((4 * count, width), BF16),
        compiler_params=params(1),
        cost_estimate=pl.CostEstimate(flops=0, bytes_accessed=2 * 10**6, transcendentals=0),
        name="collect",
    )(*arrays)


def spread_kernel(pieces, x_ref, *outs):
    place = {}
    for out_index, (first, count) in enumerate(pieces):
        for unit in range(first, first + count):
            place[unit] = (out_index, unit - first)
    for pair in range(x_ref.shape[1] // LANES):
        tile = x_ref[:, pair * LANES : (pair + 1) * LANES].astype(F32)
        packed = pack_pair(tile)
        for side in range(2):
            out_index, spot = place[2 * pair + side]
            outs[out_index][spot, 0] = packed[side].astype(BF16)


def spread(pieces, rows_array):
    rows, width = rows_array.shape
    half = rows // 2
    count = half // 2
    return pl.pallas_call(
        functools.partial(spread_kernel, pieces),
        grid=(2,),
        in_specs=[pl.BlockSpec((half, width), lambda i: (i, 0))],
        out_specs=[
            pl.BlockSpec((units, 1, count, LANES), lambda i: (0, i, 0, 0)) for _, units in pieces
        ],
        out_shape=[jax.ShapeDtypeStruct((units, 2, count, LANES), BF16) for _, units in pieces],
        compiler_params=params(1),
        cost_estimate=pl.CostEstimate(flops=0, bytes_accessed=2 * 10**6, transcendentals=0),
        name="spread",
    )(rows_array)


def turn_back(tile, cos_table, sine_table):
    near = (lane_index(tile.shape[0]) % HEAD_DIM) < HEAD_DIM // 2
    scaled = tile * sine_table
    moved = jnp.where(
        near,
        pltpu.roll(scaled, LANES - HEAD_DIM // 2, 1),
        pltpu.roll(scaled, HEAD_DIM // 2, 1),
    )
    return tile * cos_table + moved


def collect_grad_kernel(spots, c_ref, s_ref, *refs):
    ins, (q_out, k_out, v_out) = refs[:-3], refs[-3:]
    cos_table, sine_table = c_ref[...], s_ref[...]
    rows = cos_table.shape[0]
    low = lane_index(rows) < HEAD_DIM
    for pair in range(len(spots) // 2):
        cut = slice(pair * LANES, (pair + 1) * LANES)
        kvs, packed = [], []
        for side in range(2):
            array, spot = spots[2 * pair + side]
            kvs.append(ins[array][spot, 0, :rows, :].astype(F32))
            packed.append(ins[array][spot, 0, rows:, :].astype(F32))
        grad_k = jnp.where(low, kvs[0], flip(kvs[1]))
        grad_v = jnp.where(low, flip(kvs[0]), kvs[1])
        q_out[:, cut] = turn_back(unpack_pair(*packed), cos_table, sine_table).astype(BF16)
        k_out[:, cut] = turn_back(grad_k, cos_table, sine_table).astype(BF16)
        v_out[:, cut] = grad_v.astype(BF16)


def collect_grad(spots, arrays, cos_table, sine_table):
    units, _, depth, _ = arrays[0].shape
    half = depth * 2 // 3
    width = len(spots) * HEAD_DIM
    row_block = pl.BlockSpec((half, width), lambda i: (i, 0))
    table = pl.BlockSpec((half, LANES), lambda i: (i, 0))
    shape = jax.ShapeDtypeStruct((2 * half, width), BF16)
    return pl.pallas_call(
        functools.partial(collect_grad_kernel, spots),
        grid=(2,),
        in_specs=[table, table]
        + [pl.BlockSpec((units, 1, depth, LANES), lambda i: (0, i, 0, 0)) for _ in arrays],
        out_specs=[row_block] * 3,
        out_shape=[shape] * 3,
        compiler_params=params(1),
        cost_estimate=pl.CostEstimate(flops=0, bytes_accessed=6 * 10**6, transcendentals=0),
        name="collect_grad",
    )(cos_table, sine_table, *arrays)


def matmul(left, right):
    return jnp.dot(left, right, preferred_element_type=F32)


def norm_backward(grad_out, values, recip_rows, gain):
    scaled = grad_out * gain
    grad_in = recip_rows * scaled - values * (recip_rows * recip_rows * recip_rows) * jnp.mean(
        scaled * values, -1, keepdims=True
    )
    return (grad_in, jnp.sum(grad_out * values * recip_rows, 0))


def feed_forward(tokens, cotangent, attended, w_out, gain_mlp, w_gate, w_up, w_down):
    inputs = tokens.astype(F32)
    gain = gain_mlp.astype(F32)
    middle = inputs + matmul(attended, w_out)
    recip = lax.rsqrt(jnp.mean(middle * middle, -1, keepdims=True) + EPS)
    mlp_low = (middle * recip * gain).astype(BF16)
    gate_pre = matmul(mlp_low, w_gate)
    up_pre = matmul(mlp_low, w_up)
    gate_sigmoid = jax.nn.sigmoid(gate_pre)
    silu_value = gate_pre * gate_sigmoid
    hidden_low = (silu_value * up_pre).astype(BF16)
    result = (middle + matmul(hidden_low, w_down)).astype(BF16)
    grad_hidden = jnp.einsum("td,fd->tf", cotangent, w_down, preferred_element_type=F32)
    grad_gate = (
        grad_hidden * up_pre * gate_sigmoid * (1.0 + gate_pre * (1.0 - gate_sigmoid))
    ).astype(BF16)
    grad_up = (grad_hidden * silu_value).astype(BF16)
    grad_normed = jnp.einsum(
        "tf,df->td", grad_gate, w_gate, preferred_element_type=F32
    ) + jnp.einsum("tf,df->td", grad_up, w_up, preferred_element_type=F32)
    grad_mid, grad_gain = norm_backward(grad_normed, middle, recip, gain)
    grad_middle = cotangent.astype(F32) + grad_mid
    grad_branch = grad_middle.astype(BF16)
    grad_att = jnp.einsum("te,de->td", grad_branch, w_out, preferred_element_type=F32).astype(BF16)
    return result, grad_middle, grad_att, grad_gain, (
        (attended, grad_branch),
        (mlp_low, grad_gate),
        (mlp_low, grad_up),
        (hidden_low, cotangent),
    )


def outer_sum(pairs):
    total = None
    for left, right in pairs:
        part = jnp.einsum("td,te->de", left, right, preferred_element_type=F32)
        total = part if total is None else total + part
    return total


def body(
    tokens, cotangent, doc_lengths, gain_attn, w_query, w_key, w_value, w_out, gain_mlp, w_gate, w_up, w_down
):
    micros, _, rows, width = tokens.shape
    heads = width // HEAD_DIM
    devices = lax.axis_size("ctx")
    place = lax.axis_index("ctx")
    chips = devices // 2
    core = place % 2
    half = rows // 2
    units = micros * heads
    rounds = -(-units // chips)
    swap = [(i, i ^ 1) for i in range(devices)]

    def gathered(shard):
        return lax.all_gather(shard, "fsdp", axis=0, tiled=True)

    gain_attn, w_query, w_key, w_value, w_out, gain_mlp, w_gate, w_up, w_down = (
        gathered(shard)
        for shard in (gain_attn, w_query, w_key, w_value, w_out, gain_mlp, w_gate, w_up, w_down)
    )
    lengths = doc_lengths[:, 0]
    doc_ends = jnp.cumsum(lengths, -1)
    starts = (doc_ends - lengths).astype(jnp.int32)

    def begins_of(micro_starts, positions):
        reached = positions[:, None] >= micro_starts[None, :]
        return jnp.max(jnp.where(reached, micro_starts[None, :], 0), -1)

    lane = jnp.arange(LANES)
    inverse = jnp.power(10000.0, -(lane % (HEAD_DIM // 2)).astype(F32) / (HEAD_DIM // 2))
    sign = jnp.where((lane % HEAD_DIM) < HEAD_DIM // 2, -1.0, 1.0)
    positions = place * rows + jnp.arange(rows, dtype=jnp.int32)
    tables = []
    for micro in range(micros):
        offsets = (positions - begins_of(starts[micro], positions)).astype(F32)
        angles = offsets[:, None] * inverse[None, :]
        tables.append((jnp.cos(angles), jnp.sin(angles) * sign))

    def parts_of(micro):
        parts = []
        for turn_index in range(rounds):
            first = max(turn_index * chips, micro * heads)
            last = min((turn_index + 1) * chips, (micro + 1) * heads)
            if last > first:
                parts.append((turn_index, first - micro * heads, last - first))
        return parts

    def assemble(per_micro, tail):
        buffers = []
        for turn_index in range(rounds):
            found = [piece for piece, (index, _, _) in per_micro if index == turn_index]
            held = sum(piece.shape[0] for piece in found)
            if held < chips:
                found.append(jnp.zeros((chips - held, 2) + tail, BF16))
            whole = found[0] if len(found) == 1 else jnp.concatenate(found, 0)
            buffers.append(whole.reshape((devices,) + tail))
        return buffers

    def spots_of(micro):
        used = [index for index, _, _ in parts_of(micro)]
        spots = []
        for head in range(heads):
            unit = micro * heads + head
            spots.append((used.index(unit // chips), unit % chips))
        return used, tuple(spots)

    def exchange(buffer):
        return lax.all_to_all(buffer, "ctx", split_axis=0, concat_axis=0, tiled=True)

    normed, sends = [], []
    for micro in range(micros):
        parts = parts_of(micro)
        outs = project(
            tuple((first, count) for _, first, count in parts),
            tokens[micro, 0],
            gain_attn[None, :],
            *tables[micro],
            w_query,
            w_key,
            w_value,
        )
        normed.append(outs[0])
        sends += list(zip(outs[1:], parts))
    depth = half + half // 2
    received = [exchange(buffer) for buffer in assemble(sends, (depth, LANES))]

    block_first = jnp.arange(devices, dtype=jnp.int32) * rows + core * half
    infos, unit_starts, others, attended_back, kept = [], [], [], [], []
    for turn_index in range(rounds):
        unit = turn_index * chips + place // 2
        chosen = lax.dynamic_index_in_dim(
            starts, jnp.minimum(unit // heads, micros - 1), 0, keepdims=False
        )
        lowest = begins_of(chosen, block_first) // rows
        inner = -(-begins_of(chosen, block_first + half - 1) // rows)
        block = jnp.arange(devices, dtype=jnp.int32)
        live = unit < units
        lowest = jnp.where(live, lowest, block)
        inner = jnp.where(live, jnp.minimum(inner, block), block)
        info = jnp.concatenate([core[None], jnp.stack([lowest, inner], 1).reshape(-1)])
        infos.append(info.astype(jnp.int32))
        unit_starts.append(chosen)
        other = lax.ppermute(received[turn_index], "ctx", swap)
        others.append(other)
        out, lse = attend(infos[-1], chosen, received[turn_index], other)
        kept.append((out, lse))
        attended_back.append(exchange(out).reshape(chips, 2, half // 2, LANES))

    results, grad_middles, mid_pairs, grad_gain_mlp, grad_sends = [], [], [], 0.0, []
    for micro in range(micros):
        used, spots = spots_of(micro)
        attended = collect(spots, [attended_back[index] for index in used])
        result, grad_middle, grad_att, grad_gain, pairs = feed_forward(
            tokens[micro, 0], cotangent[micro, 0], attended, w_out, gain_mlp, w_gate, w_up, w_down
        )
        results.append(result)
        grad_middles.append(grad_middle)
        mid_pairs.append(pairs)
        grad_gain_mlp = grad_gain_mlp + grad_gain
        parts = parts_of(micro)
        outs = spread(tuple((first, count) for _, first, count in parts), grad_att)
        grad_sends += list(zip(outs, parts))
    grads_in = [exchange(buffer) for buffer in assemble(grad_sends, (half // 2, LANES))]

    def reduced(full):
        part = lax.psum_scatter(full.astype(BF16), "fsdp", scatter_dimension=0, tiled=True)
        return part

    grad_w_out, grad_w_gate, grad_w_up, grad_w_down = (
        reduced(outer_sum([pairs[index] for pairs in mid_pairs])) for index in range(4)
    )

    grad_back = []
    for turn_index in range(rounds):
        own, away = attend_grad(
            infos[turn_index],
            unit_starts[turn_index],
            received[turn_index],
            others[turn_index],
            grads_in[turn_index],
            *kept[turn_index],
        )
        back = lax.ppermute(away, "ctx", swap)
        own_kv = (own[:, :half].astype(F32) + back.astype(F32)).astype(BF16)
        buffer = jnp.concatenate([own_kv, own[:, half:]], 1)
        grad_back.append(exchange(buffer).reshape(chips, 2, depth, LANES))

    grad_inputs, grad_pairs, grad_gain_attn = [], [], 0.0
    for micro in range(micros):
        used, spots = spots_of(micro)
        grad_q, grad_k, grad_v = collect_grad(
            spots, [grad_back[index] for index in used], *tables[micro]
        )
        grad_normed = (
            jnp.einsum("te,de->td", grad_q, w_query, preferred_element_type=F32)
            + jnp.einsum("te,de->td", grad_k, w_key, preferred_element_type=F32)
            + jnp.einsum("te,de->td", grad_v, w_value, preferred_element_type=F32)
        )
        inputs = tokens[micro, 0].astype(F32)
        recip = lax.rsqrt(jnp.mean(inputs * inputs, -1, keepdims=True) + EPS)
        grad_in, grad_gain = norm_backward(grad_normed, inputs, recip, gain_attn.astype(F32))
        grad_inputs.append((grad_middles[micro] + grad_in).astype(BF16))
        grad_gain_attn = grad_gain_attn + grad_gain
        grad_pairs.append(
            ((normed[micro], grad_q), (normed[micro], grad_k), (normed[micro], grad_v))
        )
    grad_w_query, grad_w_key, grad_w_value = (
        reduced(outer_sum([pairs[index] for pairs in grad_pairs])) for index in range(3)
    )
    grads = (
        reduced(grad_gain_attn),
        grad_w_query,
        grad_w_key,
        grad_w_value,
        grad_w_out,
        reduced(grad_gain_mlp),
        grad_w_gate,
        grad_w_up,
        grad_w_down,
    )
    totals = [lax.psum(part, "ctx").astype(F32) for part in grads]
    return (jnp.stack(results)[:, None], jnp.stack(grad_inputs)[:, None], *totals)


def solution(mesh):
    weight, gain = P("fsdp", None), P("fsdp")
    rows = P(None, "fsdp", "ctx", None)
    weights = (gain, weight, weight, weight, weight, gain, weight, weight, weight)
    return jax.shard_map(
        body,
        mesh=mesh,
        in_specs=(rows, rows, P(None, "fsdp", None)) + weights,
        out_specs=(rows, rows) + weights,
        check_vma=False,
    )
```

time: 2960 us -> 978 us (0.33)
  starting transfers between devices: 1620 us -> 79.8 us
  Pallas kernels: 0 us -> 277 us
  waiting for transfers between devices: 653 us -> 384 us
  other arithmetic: 202 us -> 37.6 us
  local copies, waits for them, and re-layouts: 155 us -> 21.5 us
  matrix products: 204 us -> 99 us
  loops' own time: 44.1 us -> 0 us
    ppermute x100 -> x6, starting transfers between devices: 1620 us -> 1.55 us  [the longest x3 1.54 us: body(): other = lax.ppermute(received[turn_index], 'ctx', swap)]
    reduce_scatter x14 -> x7, waiting for transfers between devices: 335 us -> 56.1 us  [reduced(): lax.psum_scatter(full.astype(BF16), 'fsdp', scatter_dimension=0, tiled=True)]
    pallas_call x0 -> x14, Pallas kernels: none -> 277 us  [the longest x3 131 us: attend_grad(): pl.pallas_call(attend_grad_kernel, grid_spec=pltpu.PrefetchScalarGridSpec...]
    all_to_all x0 -> x12, waiting for transfers between devices: none -> 143 us  [exchange(): lax.all_to_all(buffer, 'ctx', split_axis=0, concat_axis=0, tiled=True)]
    add x62 -> x3, other arithmetic: 134 us -> 0.94 us  [the longest x1 0.93 us: feed_forward(): grad_middle = cotangent.astype(F32) + grad_mid]
    dot_general x60 -> x36, matrix products: 204 us -> 99 us  [the longest x14 32.5 us: outer_sum(): part = jnp.einsum('td,te->de', left, right, preferred_element_type=F32)]
    ppermute x100 -> x6, waiting for transfers between devices: 98.2 us -> 1.8 us  [the longest x3 1.79 us: body(): back = lax.ppermute(away, 'ctx', swap)]
    while x454 -> x0, local copies, waits for them, and re-layouts: 92.3 us -> none
  transfers between devices with their start and end apart: 129 -> 33, of which waited for: 54 -> 16; matrix products, arithmetic and copies ran while one was open for 15% -> 10% of each run, Pallas kernels for 0% -> 27%
where the time goes in v1:
time: 978 us; the launch traced here: 964 us
  waiting for transfers between devices  384 us (39%)
  Pallas kernels  277 us (28%)
  matrix products  99 us (10%)
  starting transfers between devices  79.8 us (8%)
  blocking collectives  48.9 us (5%)
  other arithmetic  37.6 us (4%)
  local copies, waits for them, and re-layouts  21.5 us (2%)
  between operations  16.2 us (2%)
    all_to_all x12, waiting for transfers between devices, exchange(): lax.all_to_all(buffer, 'ctx', split_axis=0, concat_axis=0, tiled=True)  143 us
    pallas_call x3, Pallas kernels, attend_grad(): pl.pallas_call(attend_grad_kernel, grid_spec=pltpu.PrefetchScalarGridSpec...  131 us
    pallas_call x3, Pallas kernels, attend(): pl.pallas_call(attend_kernel, grid_spec=pltpu.PrefetchScalarGridSpec(num_...  113 us
    psum x1, waiting for transfers between devices, body(): totals = [lax.psum(part, 'ctx').astype(F32) for part in grads]  100 us
    all_gather x7, waiting for transfers between devices, gathered(): return lax.all_gather(shard, 'fsdp', axis=0, tiled=True)  78 us
    all_to_all x12, starting transfers between devices, exchange(): lax.all_to_all(buffer, 'ctx', split_axis=0, concat_axis=0, tiled=True)  76.8 us
    reduce_scatter x7, waiting for transfers between devices, reduced(): lax.psum_scatter(full.astype(BF16), 'fsdp', scatter_dimension=0, tiled=True)  56.1 us
    psum x1, blocking collectives, body(): totals = [lax.psum(part, 'ctx').astype(F32) for part in grads]  34 us
  transfers between devices with their start and end apart: 33, of which 16 were waited for; matrix products, arithmetic and copies ran while one was open for 10% of the time, Pallas kernels for 27%

profile of v1, /device:TPU:0, one launch (start us, length us, event | category | flops | bytes accessed | tf_op | source)
XLA Modules:
  0.0 963.8 jit_solution(7954560390435101663)
XLA Ops:
  19.6 15.5 %all-gather.10.cloned.1.call-done.wq_ref = bf16[768,768]{1,0:T(8,128)(2,1)} async-done(((bf16[384,768]{1,0:T(8,128)(2,1)}), bf16[768,768]{1,0:T(8,128)(2,1)}) %all-gather.10.cloned.1.call-update) | async-done | bytes 1179664 | tf_op jit(solution)/shard_map/all_gather | solution.py:490
  35.1 24.3 %all-gather.12.cloned.1.call-done.wk_ref = bf16[768,768]{1,0:T(8,128)(2,1)} async-done(((bf16[384,768]{1,0:T(8,128)(2,1)}), bf16[768,768]{1,0:T(8,128)(2,1)}) %all-gather.12.cloned.1.call-update) | async-done | bytes 1179664 | tf_op jit(solution)/shard_map/all_gather | solution.py:490
  59.4 24.3 %all-gather.14.cloned.1.call-done.wv_ref = bf16[768,768]{1,0:T(8,128)(2,1)} async-done(((bf16[384,768]{1,0:T(8,128)(2,1)}), bf16[768,768]{1,0:T(8,128)(2,1)}) %all-gather.14.cloned.1.call-update) | async-done | bytes 1179664 | tf_op jit(solution)/shard_map/all_gather | solution.py:490
  105.6 31.3 %all-to-all-done.2.mine = bf16[16,384,128]{2,1,0:T(8,128)(2,1)S(1)} async-done(((bf16[16,384,128]{2,1,0:T(8,128)(2,1)}), bf16[16,384,128]{2,1,0:T(8,128)(2,1)S(1)}, u32[]{:S(2)}, u32[]{:S(2)}) %all-to-all-start.2) | async-done | bytes 1572896 | tf_op jit(solution)/shard_map/all_to_all | solution.py:543
  136.8 9.2 all-to-all-start.4
  146.6 31.3 %all-to-all-done.4.mine = bf16[16,384,128]{2,1,0:T(8,128)(2,1)} async-done(((bf16[16,384,128]{2,1,0:T(8,128)(2,1)}), bf16[16,384,128]{2,1,0:T(8,128)(2,1)}, u32[]{:S(2)}, u32[]{:S(2)}) %all-to-all-start.4) | async-done | bytes 1572896 | tf_op jit(solution)/shard_map/all_to_all | solution.py:543
  177.9 9.2 all-to-all-start
  190.8 28.2 %all-to-all-done.mine = bf16[16,384,128]{2,1,0:T(8,128)(2,1)} async-done(((bf16[16,384,128]{2,1,0:T(8,128)(2,1)}), bf16[16,384,128]{2,1,0:T(8,128)(2,1)}, u32[]{:S(2)}, u32[]{:S(2)}) %all-to-all-start) | async-done | bytes 1572896 | tf_op jit(solution)/shard_map/all_to_all | solution.py:543
  219.9 37.7 %attend.4 = (bf16[16,128,128]{2,1,0:T(8,128)(2,1)}, f32[16,1,256]{2,1,0:T(1,128)}) custom-call(s32[33]{0:T(128)} %pad_add_fusion.4.info, s32[8]{0:T(128)} %copy-done.63, bf16[16,384,128]{2,1,0:T(8,128)(2,1)} %copy-done.31, bf16[16,384,128]{2,1,0:T(8,128)(2,1)} %collective-permute-done.1.other), custom_call_target="tpu_custom_call" | custom-call | flops 16000000000 | bytes 10000000 | tf_op jit(solution)/shard_map/attend/pallas_call | solution.py:188
  257.6 8.6 all-to-all-start.3
  266.2 37.7 %attend.5 = (bf16[16,128,128]{2,1,0:T(8,128)(2,1)}, f32[16,1,256]{2,1,0:T(1,128)}) custom-call(s32[33]{0:T(128)} %pad_add_fusion.5.info, s32[8]{0:T(128)} %copy-done.62, bf16[16,384,128]{2,1,0:T(8,128)(2,1)} %all-to-all-done.4.mine, bf16[16,384,128]{2,1,0:T(8,128)(2,1)} %collective-permute-done.2.other), custom_call_target="tpu_custom_call" | custom-call | flops 16000000000 | bytes 10000000 | tf_op jit(solution)/shard_map/attend/pallas_call | solution.py:188
  310.0 37.7 %attend.3 = (bf16[16,128,128]{2,1,0:T(8,128)(2,1)}, f32[16,1,256]{2,1,0:T(1,128)}) custom-call(s32[33]{0:T(128)} %pad_add_fusion.3.info, s32[8]{0:T(128)} %copy-done.61, bf16[16,384,128]{2,1,0:T(8,128)(2,1)} %all-to-all-done.mine, bf16[16,384,128]{2,1,0:T(8,128)(2,1)} %collective-permute-done.other), custom_call_target="tpu_custom_call" | custom-call | flops 16000000000 | bytes 10000000 | tf_op jit(solution)/shard_map/attend/pallas_call | solution.py:188
  387.5 13.9 %all-gather.22.cloned.1.call-done = bf16[2048,768]{1,0:T(8,128)(2,1)} async-done(((bf16[1024,768]{1,0:T(8,128)(2,1)}), bf16[2048,768]{1,0:T(8,128)(2,1)}) %all-gather.22.cloned.1.call-update) | async-done | bytes 3145744 | tf_op jit(solution)/shard_map/all_gather | solution.py:490
  401.4 7.4 multiply_convert_fusion.2
  471.0 8.2 all-to-all-done.8.do_ref
  484.2 43.5 %attend_grad.4 = (bf16[16,384,128]{2,1,0:T(8,128)(2,1)}, bf16[16,256,128]{2,1,0:T(8,128)(2,1)}) custom-call(s32[33]{0:T(128)} %pad_add_fusion.4.info, s32[8]{0:T(128)} %copy-done.63, bf16[16,384,128]{2,1,0:T(8,128)(2,1)} %copy-done.31, bf16[16,384,128]{2,1,0:T(8,128)(2,1)} %collective-permute-done.1.other, bf16[16,128,128]{2,1,0:T(8,128)(2,1)} %copy-done.55, ...), custom_call_target="tpu_custom_call" | custom-call | flops 32000000000 | bytes 10000000 | tf_op jit(solution)/shard_map/attend_grad/pallas_call | solution.py:285
  537.3 11.6 %all-to-all-done.6.do_ref = bf16[16,128,128]{2,1,0:T(8,128)(2,1)S(1)} async-done(((bf16[16,128,128]{2,1,0:T(8,128)(2,1)}), bf16[16,128,128]{2,1,0:T(8,128)(2,1)S(1)}, u32[]{:S(2)}, u32[]{:S(2)}) %all-to-all-start.6) | async-done | bytes 524320 | tf_op jit(solution)/shard_map/all_to_all | solution.py:543
  554.2 43.7 %attend_grad.5 = (bf16[16,384,128]{2,1,0:T(8,128)(2,1)}, bf16[16,256,128]{2,1,0:T(8,128)(2,1)}) custom-call(s32[33]{0:T(128)} %pad_add_fusion.5.info, s32[8]{0:T(128)} %copy-done.62, bf16[16,384,128]{2,1,0:T(8,128)(2,1)} %all-to-all-done.4.mine, bf16[16,384,128]{2,1,0:T(8,128)(2,1)} %collective-permute-done.2.other, bf16[16,128,128]{2,1,0:T(8,128)(2,1)} %copy-done.54, ...), custom_call_target="tpu_custom_call" | custom-call | flops 32000000000 | bytes 10000000 | tf_op jit(solution)/shard_map/attend_grad/pallas_call | solution.py:285
  616.8 43.5 %attend_grad.3 = (bf16[16,384,128]{2,1,0:T(8,128)(2,1)}, bf16[16,256,128]{2,1,0:T(8,128)(2,1)}) custom-call(s32[33]{0:T(128)} %pad_add_fusion.3.info, s32[8]{0:T(128)} %copy-done.61, bf16[16,384,128]{2,1,0:T(8,128)(2,1)} %all-to-all-done.mine, bf16[16,384,128]{2,1,0:T(8,128)(2,1)} %collective-permute-done.other, bf16[16,128,128]{2,1,0:T(8,128)(2,1)} %copy-done.53, ...), custom_call_target="tpu_custom_call" | custom-call | flops 32000000000 | bytes 10000000 | tf_op jit(solution)/shard_map/attend_grad/pallas_call | solution.py:285
  677.9 25.9 %all-to-all-done.7 = bf16[16,384,128]{2,1,0:T(8,128)(2,1)S(1)} async-done(((bf16[16,384,128]{2,1,0:T(8,128)(2,1)}), bf16[16,384,128]{2,1,0:T(8,128)(2,1)S(1)}, u32[]{:S(2)}, u32[]{:S(2)}) %all-to-all-start.7) | async-done | bytes 1572896 | tf_op jit(solution)/shard_map/all_to_all | solution.py:543
  740.2 24.7 %reduce-scatter.10.cloned.1.call-done = bf16[384,768]{1,0:T(8,128)(2,1)} async-done(((bf16[768,768]{1,0:T(8,128)(2,1)}), bf16[384,768]{1,0:T(8,128)(2,1)}) %reduce-scatter.10.cloned.1.call-update) | async-done | bytes 589840 | tf_op jit(solution)/shard_map/reduce_scatter | solution.py:601
  764.9 24.5 %reduce-scatter.12.cloned.1.call-done = bf16[384,768]{1,0:T(8,128)(2,1)} async-done(((bf16[768,768]{1,0:T(8,128)(2,1)}), bf16[384,768]{1,0:T(8,128)(2,1)}) %reduce-scatter.12.cloned.1.call-update) | async-done | bytes 589840 | tf_op jit(solution)/shard_map/reduce_scatter | solution.py:601
  805.7 34.0 %all-reduce.2 = (bf16[384]{0:T(512)(128)(2,1)S(1)}, bf16[384]{0:T(512)(128)(2,1)S(1)}) all-reduce(bf16[384]{0:T(512)(128)(2,1)S(1)} %dynamic-slice.1, bf16[384]{0:T(512)(128)(2,1)S(1)} %dynamic-slice.3), channel_id=1, replica_groups=mesh['ctx'=16,'fsdp'=2] {'ctx'}, use_global_device_ids=true, to_apply=%region_20.21 | all-reduce | flops 768 | bytes 3072 | tf_op jit(solution)/shard_map/psum | solution.py:656
  845.1 100.2 %all-reduce.7.cloned.1.call-done = (bf16[384,768]{1,0:T(8,128)(2,1)}, bf16[384,768]{1,0:T(8,128)(2,1)}, bf16[384,768]{1,0:T(8,128)(2,1)}, bf16[384,768]{1,0:T(8,...) async-done(((bf16[384,768]{1,0:T(8,128)(2,1)}, bf16[384,768]{1,0:T(8,128)(2,1)}, bf16[384,768]{1,0:T(8,128)(2,1)}, ...) | async-done | bytes 7077904 | tf_op jit(solution)/shard_map/psum | solution.py:656
  (344 shorter events, 271.7 us)
Async XLA Ops:
  7.9 51.5 %all-gather.12.cloned.1.call-start = ((), (), s32[]{:S(2)}) async-start(), calls=%async_computation.20 | async-start | bytes 1769472 | tf_op jit(solution)/shard_map/all_gather | solution.py:490
  8.7 75.0 %all-gather.14.cloned.1.call-start = ((), (), s32[]{:S(2)}) async-start(), calls=%async_computation.21 | async-start | bytes 1769472 | tf_op jit(solution)/shard_map/all_gather | solution.py:490
  105.0 266.0 %all-gather.16.cloned.1.call-start = ((), (), s32[]{:S(2)}) async-start(), calls=%async_computation.22 | async-start | bytes 1769472 | tf_op jit(solution)/shard_map/all_gather | solution.py:490
  136.8 41.1 %all-to-all-start.4 = ((bf16[16,384,128]{2,1,0:T(8,128)(2,1)}), bf16[16,384,128]{2,1,0:T(8,128)(2,1)}, u32[]{:S(2)}, u32[]{:S(2)}) async-start(bf16[16,384,128]{2,1,0:T(8,128)(2,1)} %bitcast.212), calls=%async_computation.4 | async-start | bytes 3145728 | tf_op jit(solution)/shard_map/all_to_all | solution.py:543
  146.0 229.7 %all-gather.18.cloned.1.call-start = ((), (), s32[]{:S(2)}) async-start(), calls=%async_computation.23 | async-start | bytes 4718592 | tf_op jit(solution)/shard_map/all_gather | solution.py:490
  177.9 41.1 %all-to-all-start = ((bf16[16,384,128]{2,1,0:T(8,128)(2,1)}), bf16[16,384,128]{2,1,0:T(8,128)(2,1)}, u32[]{:S(2)}, u32[]{:S(2)}) async-start(bf16[16,384,128]{2,1,0:T(8,128)(2,1)} %bitcast.211), calls=%async_computation | async-start | bytes 3145728 | tf_op jit(solution)/shard_map/all_to_all | solution.py:543
  187.1 194.6 %all-gather.20.cloned.1.call-start = ((), (), s32[]{:S(2)}) async-start(), calls=%async_computation.24 | async-start | bytes 4718592 | tf_op jit(solution)/shard_map/all_gather | solution.py:490
  190.0 76.2 %collective-permute-start.2 = (bf16[16,384,128]{2,1,0:T(8,128)(2,1)}, bf16[16,384,128]{2,1,0:T(8,128)(2,1)}, u32[]{:S(2)}, u32[]{:S(2)}) collective-permute-start(bf16[16,384,128]{2,1,0:T(8,128)(2,1)} %all-to-all-done.4.mine), channel_id=1, source_target_pairs={{0,2},{2,0},{4,6},{6,4},{8,10},{10,8},{12,14},{14,12},{16,18},{18,... | collective-permute-start | bytes 4718600 | tf_op jit(solution)/shard_map/ppermute | solution.py:578
  219.0 91.0 %collective-permute-start = (bf16[16,384,128]{2,1,0:T(8,128)(2,1)}, bf16[16,384,128]{2,1,0:T(8,128)(2,1)}, u32[]{:S(2)}, u32[]{:S(2)}) collective-permute-start(bf16[16,384,128]{2,1,0:T(8,128)(2,1)} %all-to-all-done.mine), channel_id=1, source_target_pairs={{0,2},{2,0},{4,6},{6,4},{8,10},{10,8},{12,14},{14,12},{16,18},{18,... | collective-permute-start | bytes 4718600 | tf_op jit(solution)/shard_map/ppermute | solution.py:578
  257.6 46.3 %all-to-all-start.3 = ((bf16[16,128,128]{2,1,0:T(8,128)(2,1)}), bf16[16,128,128]{2,1,0:T(8,128)(2,1)S(1)}, u32[]{:S(2)}, u32[]{:S(2)}) async-start(bf16[16,128,128]{2,1,0:T(8,128)(2,1)} %get-tuple-element.43.o_ref), calls=%async_computation.3 | async-start | bytes 1048576 | tf_op jit(solution)/shard_map/all_to_all | solution.py:543
  303.9 43.7 %all-to-all-start.5 = ((bf16[16,128,128]{2,1,0:T(8,128)(2,1)}), bf16[16,128,128]{2,1,0:T(8,128)(2,1)S(1)}, u32[]{:S(2)}, u32[]{:S(2)}) async-start(bf16[16,128,128]{2,1,0:T(8,128)(2,1)} %get-tuple-element.45.o_ref), calls=%async_computation.5 | async-start | bytes 1048576 | tf_op jit(solution)/shard_map/all_to_all | solution.py:543
  353.7 47.7 %all-gather.22.cloned.1.call-start = ((), (), s32[]{:S(2)}) async-start(), calls=%async_computation.25 | async-start | bytes 4718592 | tf_op jit(solution)/shard_map/all_gather | solution.py:490
  354.5 378.8 %reduce-scatter.14.cloned.1.call-start = ((), (), s32[]{:S(2)}) async-start(), calls=%async_computation.29 | async-start | bytes 1769472 | tf_op jit(solution)/shard_map/reduce_scatter | solution.py:601
  439.5 293.8 %reduce-scatter.16.cloned.1.call-start = ((), (), s32[]{:S(2)}) async-start(), calls=%async_computation.30 | async-start | bytes 4718592 | tf_op jit(solution)/shard_map/reduce_scatter | solution.py:601
  464.9 268.3 %reduce-scatter.18.cloned.1.call-start = ((), (), s32[]{:S(2)}) async-start(), calls=%async_computation.31 | async-start | bytes 4718592 | tf_op jit(solution)/shard_map/reduce_scatter | solution.py:601
  480.0 47.7 %all-to-all-start.10 = ((bf16[16,128,128]{2,1,0:T(8,128)(2,1)}), bf16[16,128,128]{2,1,0:T(8,128)(2,1)S(1)}, u32[]{:S(2)}, u32[]{:S(2)}) async-start(bf16[16,128,128]{2,1,0:T(8,128)(2,1)} %bitcast.33), calls=%async_computation.10 | async-start | bytes 1048576 | tf_op jit(solution)/shard_map/all_to_all | solution.py:543
  549.7 59.8 %all-to-all-start.9 = ((bf16[16,384,128]{2,1,0:T(8,128)(2,1)}), bf16[16,384,128]{2,1,0:T(8,128)(2,1)S(1)}, u32[]{:S(2)}, u32[]{:S(2)}) async-start(bf16[16,384,128]{2,1,0:T(8,128)(2,1)} %pad_maximum_fusion.2), calls=%async_computation.9 | async-start | bytes 3145728 | tf_op jit(solution)/shard_map/all_to_all | solution.py:543
  553.9 179.4 %reduce-scatter.20.cloned.1.call-start = ((), (), s32[]{:S(2)}) async-start(), calls=%async_computation.32 | async-start | bytes 4718592 | tf_op jit(solution)/shard_map/reduce_scatter | solution.py:601
  610.7 55.3 %all-to-all-start.11 = ((bf16[16,384,128]{2,1,0:T(8,128)(2,1)}), bf16[16,384,128]{2,1,0:T(8,128)(2,1)S(1)}, u32[]{:S(2)}, u32[]{:S(2)}) async-start(bf16[16,384,128]{2,1,0:T(8,128)(2,1)} %pad_maximum_fusion.3), calls=%async_computation.11 | async-start | bytes 3145728 | tf_op jit(solution)/shard_map/all_to_all | solution.py:543
  665.9 37.9 %all-to-all-start.7 = ((bf16[16,384,128]{2,1,0:T(8,128)(2,1)}), bf16[16,384,128]{2,1,0:T(8,128)(2,1)S(1)}, u32[]{:S(2)}, u32[]{:S(2)}) async-start(bf16[16,384,128]{2,1,0:T(8,128)(2,1)} %pad_maximum_fusion.1), calls=%async_computation.7 | async-start | bytes 3145728 | tf_op jit(solution)/shard_map/all_to_all | solution.py:543
  672.0 68.2 %reduce-scatter.8.cloned.1.call-start = ((), (), s32[]{:S(2)}) async-start(), calls=%async_computation.26 | async-start | bytes 1769472 | tf_op jit(solution)/shard_map/reduce_scatter | solution.py:601
  714.7 50.2 %reduce-scatter.10.cloned.1.call-start = ((), (), s32[]{:S(2)}) async-start(), calls=%async_computation.27 | async-start | bytes 1769472 | tf_op jit(solution)/shard_map/reduce_scatter | solution.py:601
  718.8 70.6 %reduce-scatter.12.cloned.1.call-start = ((), (), s32[]{:S(2)}) async-start(), calls=%async_computation.28 | async-start | bytes 1769472 | tf_op jit(solution)/shard_map/reduce_scatter | solution.py:601
  722.9 222.4 %all-reduce.7.cloned.1.call-start = ((), (), s32[]{:S(2)}) async-start(), calls=%async_computation.33 | async-start | bytes 14155776 | tf_op jit(solution)/shard_map/psum | solution.py:656
  (90 other events, 1150.9 us)
Sparse Core Ops, SparseCore 0:
  9.6 25.4 all-gather.9
  36.6 22.7 all-gather.11
  60.9 22.7 all-gather.13
  107.0 23.1 all-gather.15
  148.1 45.2 all-gather.17
  194.7 44.8 all-gather.19
  356.1 45.2 all-gather.21
  439.6 21.8 reduce-scatter.13
  464.3 43.4 reduce-scatter.15
  510.4 43.4 reduce-scatter.17
  605.4 43.9 reduce-scatter.19
  714.8 25.3 reduce-scatter.7
  743.0 21.8 reduce-scatter.9
  767.5 21.8 reduce-scatter.11
  793.8 151.3 all-reduce.6

commit v2 on v1

v2 whole, which is shorter than its diff:
```python
import functools
import math

import jax
import jax.numpy as jnp
from jax import lax
from jax.experimental import pallas as pl
from jax.experimental.pallas import tpu as pltpu
from jax.sharding import PartitionSpec as P

HEAD_DIM = 64
LANES = 128
EPS = 1e-05
NEG = -1e30
LOG2E = math.log2(math.e)
LN2 = math.log(2.0)
F32 = jnp.float32
BF16 = jnp.bfloat16


def dot_nt(left, right):
    return lax.dot_general(left, right, (((1,), (1,)), ((), ())), preferred_element_type=F32)


def dot_nn(left, right):
    return lax.dot_general(left, right, (((1,), (0,)), ((), ())), preferred_element_type=F32)


def dot_tn(left, right):
    return lax.dot_general(left, right, (((0,), (0,)), ((), ())), preferred_element_type=F32)


def lane_index(rows):
    return lax.broadcasted_iota(jnp.int32, (rows, LANES), 1)


def flip(tile):
    return pltpu.roll(tile, HEAD_DIM, 1)


def params(count):
    return pltpu.CompilerParams(
        dimension_semantics=("arbitrary",) * count, vmem_limit_bytes=60 * 1024 * 1024
    )


def full_block(shape):
    zeros = (0,) * len(shape)
    return pl.BlockSpec(shape, lambda *_: zeros)


def pack_pair(tile):
    count = tile.shape[0] // 2
    low = lane_index(count) < HEAD_DIM
    top, bottom = tile[:count], tile[count:]
    return (jnp.where(low, top, flip(bottom)), jnp.where(low, flip(top), bottom))


def unpack_pair(first, second):
    low = lane_index(first.shape[0]) < HEAD_DIM
    top = jnp.where(low, first, flip(second))
    bottom = jnp.where(low, flip(first), second)
    return jnp.concatenate([top, bottom], 0)


def turn(tile):
    near = (lane_index(tile.shape[0]) % HEAD_DIM) < HEAD_DIM // 2
    return jnp.where(
        near, pltpu.roll(tile, LANES - HEAD_DIM // 2, 1), pltpu.roll(tile, HEAD_DIM // 2, 1)
    )


def project_kernel(count, n_ref, c_ref, s_ref, w_ref, out):
    joined = dot_nn(n_ref[...], w_ref[...])
    cos_table, sine_table = c_ref[...], s_ref[...]
    rows = n_ref.shape[0]
    span = count * HEAD_DIM
    low = lane_index(rows) < HEAD_DIM
    for pair in range(count // 2):
        first = pair * LANES
        q2, k2, v2 = (joined[:, part * span + first : part * span + first + LANES] for part in range(3))
        q2 = (q2 * cos_table + turn(q2) * sine_table) * (LOG2E * HEAD_DIM**-0.5)
        k2 = k2 * cos_table + turn(k2) * sine_table
        packed = pack_pair(q2)
        kv = (jnp.where(low, k2, flip(v2)), jnp.where(low, flip(k2), v2))
        for side in range(2):
            out[2 * pair + side, 0, :rows, :] = kv[side].astype(BF16)
            out[2 * pair + side, 0, rows:, :] = packed[side].astype(BF16)
    if count < out.shape[0]:
        out[count:] = jnp.zeros((out.shape[0] - count,) + out.shape[1:], BF16)


def project(span, count, micros, normed, cos_table, sine_table, weight):
    rows, width = normed.shape
    half = rows // (2 * micros)
    depth = half + half // 2
    return pl.pallas_call(
        functools.partial(project_kernel, count),
        grid=(micros, 2),
        in_specs=[
            pl.BlockSpec((half, width), lambda m, i: (2 * m + i, 0)),
            pl.BlockSpec((half, LANES), lambda m, i: (2 * m + i, 0)),
            pl.BlockSpec((half, LANES), lambda m, i: (2 * m + i, 0)),
            full_block(weight.shape),
        ],
        out_specs=pl.BlockSpec((span, 1, depth, LANES), lambda m, i: (m, i, 0, 0)),
        out_shape=jax.ShapeDtypeStruct((micros * span, 2, depth, LANES), BF16),
        compiler_params=params(2),
        cost_estimate=pl.CostEstimate(
            flops=2 * rows * width * weight.shape[1], bytes_accessed=4 * rows * width, transcendentals=0
        ),
        name="project",
    )(normed, cos_table, sine_table, weight)


def row_begins(starts_ref, positions):
    begins = jnp.zeros_like(positions)
    for index in range(starts_ref.shape[0]):
        start = starts_ref[index]
        begins = jnp.maximum(begins, jnp.where(positions >= start, start, 0))
    return begins


def unpack_one(packed, lanes_low):
    wide = packed.astype(F32)
    low = lane_index(wide.shape[0]) < HEAD_DIM
    keep = low if lanes_low else jnp.logical_not(low)
    turned = flip(wide)
    first, second = (wide, turned) if lanes_low else (turned, wide)
    return jnp.concatenate(
        [jnp.where(keep, first, 0.0), jnp.where(keep, second, 0.0)], 0
    ).astype(BF16)


def attend_kernel(info, starts, mine, other, o_ref, lse_ref):
    block = pl.program_id(0)
    core = info[0]
    lowest, inner = info[1 + 2 * block], info[2 + 2 * block]
    rows = mine.shape[1] * 2 // 3
    low = lane_index(rows) < HEAD_DIM
    queries = unpack_one(mine[block, rows:, :], True)
    row_pos = (2 * block + core) * rows + lax.broadcasted_iota(jnp.int32, (rows, 1), 0)
    begins = row_begins(starts, row_pos)
    lane_low = lane_index(2 * rows) < HEAD_DIM
    column = lax.broadcasted_iota(jnp.int32, (1, 2 * rows), 1)
    offsets = jnp.where(column < rows, column + core * rows, column - core * rows)

    def step(masked, index, carry):
        peak, acc = carry
        kv = jnp.concatenate([mine[index, :rows, :], other[index, :rows, :]], 0)
        ones_v = jnp.where(lane_low, jnp.ones_like(kv), kv)
        scores = dot_nt(queries, kv)
        if masked:
            key_pos = offsets + index * (2 * rows)
            scores = jnp.where((key_pos >= begins) & (key_pos <= row_pos), scores, NEG)
        new_peak = jnp.maximum(peak, jnp.max(scores, -1, keepdims=True))
        weights = jnp.exp2(scores - new_peak)
        acc = acc * jnp.exp2(peak - new_peak) + dot_nn(weights.astype(BF16), ones_v)
        return (new_peak, acc)

    carry = step(True, block, (jnp.full((rows, 1), NEG, F32), jnp.zeros((rows, LANES), F32)))
    carry = lax.fori_loop(lowest, inner, functools.partial(step, True), carry)
    peak, acc = lax.fori_loop(inner, block, functools.partial(step, False), carry)
    result = acc / flip(acc)
    count = rows // 2
    small_low = lane_index(count) < HEAD_DIM
    o_ref[0] = jnp.where(small_low, flip(result[:count]), result[count:]).astype(BF16)
    lse = jnp.where(low, peak + jnp.log2(acc), 0.0)
    lse_ref[0] = jnp.transpose(lse)[0:1, :]


def attend(info, starts, mine, other):
    blocks, depth, _ = mine.shape
    rows = depth * 2 // 3
    return pl.pallas_call(
        attend_kernel,
        grid_spec=pltpu.PrefetchScalarGridSpec(
            num_scalar_prefetch=2,
            grid=(blocks,),
            in_specs=[
                pl.BlockSpec(mine.shape, lambda i, *_: (0, 0, 0)),
                pl.BlockSpec(other.shape, lambda i, *_: (0, 0, 0)),
            ],
            out_specs=[
                pl.BlockSpec((1, rows // 2, LANES), lambda i, *_: (i, 0, 0)),
                pl.BlockSpec((1, 1, rows), lambda i, *_: (i, 0, 0)),
            ],
        ),
        out_shape=[
            jax.ShapeDtypeStruct((blocks, rows // 2, LANES), BF16),
            jax.ShapeDtypeStruct((blocks, 1, rows), F32),
        ],
        compiler_params=params(1),
        cost_estimate=pl.CostEstimate(
            flops=16 * 10**9, bytes_accessed=10**7, transcendentals=10**7
        ),
        name="attend",
    )(info, starts, mine, other)


def attend_grad_kernel(
    info, starts, mine, other, do_ref, o_ref, lse_ref, dm_ref, dp_ref, acc_mine, acc_other
):
    block = pl.program_id(0)
    core = info[0]
    lowest, inner = info[1 + 2 * block], info[2 + 2 * block]
    rows = mine.shape[1] * 2 // 3
    count = rows // 2

    @pl.when(block == 0)
    def _():
        acc_mine[...] = jnp.zeros_like(acc_mine)
        acc_other[...] = jnp.zeros_like(acc_other)

    queries = unpack_one(mine[block, rows:, :], True)
    grad_out = unpack_one(do_ref[0], False)
    both = jnp.concatenate([queries, grad_out], 0)
    product = jnp.transpose(do_ref[0].astype(F32) * o_ref[0].astype(F32))
    delta = jnp.concatenate(
        [
            jnp.sum(product[:HEAD_DIM], 0, keepdims=True),
            jnp.sum(product[HEAD_DIM:], 0, keepdims=True),
        ],
        1,
    )
    lse = lse_ref[0]
    row_pos = (2 * block + core) * rows + lax.broadcasted_iota(jnp.int32, (1, rows), 1)
    begins = row_begins(starts, row_pos)
    line = lax.broadcasted_iota(jnp.int32, (2 * rows, 1), 0)
    offsets = jnp.where(line < rows, line + core * rows, line - core * rows)

    def step(masked, index, grad_q):
        kv = jnp.concatenate([mine[index, :rows, :], other[index, :rows, :]], 0)
        scores = dot_nt(kv, queries)
        weights = jnp.exp2(scores - lse)
        if masked:
            key_pos = offsets + index * (2 * rows)
            weights = jnp.where((key_pos >= begins) & (key_pos <= row_pos), weights, 0.0)
        grad_weights = dot_nt(kv, grad_out)
        grad_scores = (weights * (grad_weights - delta)).astype(BF16)
        grad_kv = dot_nn(jnp.concatenate([grad_scores, weights.astype(BF16)], 1), both)
        acc_mine[index] += grad_kv[:rows]
        acc_other[index] += grad_kv[rows:]
        return grad_q + dot_tn(grad_scores, kv)

    grad_q = step(True, block, jnp.zeros((rows, LANES), F32))
    grad_q = lax.fori_loop(lowest, inner, functools.partial(step, True), grad_q)
    grad_q = lax.fori_loop(inner, block, functools.partial(step, False), grad_q)
    grad_q = grad_q * HEAD_DIM**-0.5
    small_low = lane_index(count) < HEAD_DIM
    dm_ref[block, rows:, :] = jnp.where(small_low, grad_q[:count], flip(grad_q[count:])).astype(
        BF16
    )

    @pl.when(block == pl.num_programs(0) - 1)
    def _():
        scale = jnp.where(lane_index(rows) < HEAD_DIM, LN2, 1.0)

        def flush(index, _):
            dm_ref[index, :rows, :] = (acc_mine[index] * scale).astype(BF16)
            dp_ref[index] = (acc_other[index] * scale).astype(BF16)
            return 0

        lax.fori_loop(0, mine.shape[0], flush, 0)


def attend_grad(info, starts, mine, other, grad_out, spot, out, lse):
    blocks, depth, _ = mine.shape
    rows = depth * 2 // 3
    whole = pl.BlockSpec(mine.shape, lambda i, *_: (0, 0, 0))
    small = pl.BlockSpec((1, rows // 2, LANES), lambda i, *_: (i, 0, 0))
    return pl.pallas_call(
        attend_grad_kernel,
        grid_spec=pltpu.PrefetchScalarGridSpec(
            num_scalar_prefetch=2,
            grid=(blocks,),
            in_specs=[
                whole,
                whole,
                pl.BlockSpec((1, rows // 2, LANES), lambda i, *_: (i, spot, 0)),
                small,
                pl.BlockSpec((1, 1, rows), lambda i, *_: (i, 0, 0)),
            ],
            out_specs=[whole, pl.BlockSpec((blocks, rows, LANES), lambda i, *_: (0, 0, 0))],
            scratch_shapes=[
                pltpu.VMEM((blocks, rows, LANES), F32),
                pltpu.VMEM((blocks, rows, LANES), F32),
            ],
        ),
        out_shape=[
            jax.ShapeDtypeStruct(mine.shape, BF16),
            jax.ShapeDtypeStruct((blocks, rows, LANES), BF16),
        ],
        compiler_params=params(1),
        cost_estimate=pl.CostEstimate(
            flops=32 * 10**9, bytes_accessed=10**7, transcendentals=10**7
        ),
        name="attend_grad",
    )(info, starts, mine, other, grad_out, out, lse)


def collect_kernel(counts, *refs):
    ins, out = refs[:-1], refs[-1]
    length = out.shape[0] // 2
    pieces = [(array, first) for array in ins for first in range(0, array.shape[2], length)]
    pair = 0
    for (array, first), count in zip(pieces, counts):
        cut = slice(first, first + length)
        for spot in range(0, count, 2):
            tiles = [array[spot + side, 0, cut, :].astype(F32) for side in range(2)]
            out[:, pair * LANES : (pair + 1) * LANES] = unpack_pair(*tiles).astype(BF16)
            pair += 1


def collect(counts, micros, arrays):
    units = arrays[0].shape[0]
    length = sum(array.shape[2] for array in arrays) // len(counts)
    width = sum(counts) * HEAD_DIM
    return pl.pallas_call(
        functools.partial(collect_kernel, counts),
        grid=(micros, 2),
        in_specs=[
            pl.BlockSpec((units // micros, 1, array.shape[2], LANES), lambda m, i: (m, i, 0, 0))
            for array in arrays
        ],
        out_specs=pl.BlockSpec((2 * length, width), lambda m, i: (2 * m + i, 0)),
        out_shape=jax.ShapeDtypeStruct((micros * 4 * length, width), BF16),
        compiler_params=params(2),
        cost_estimate=pl.CostEstimate(flops=0, bytes_accessed=4 * 10**6, transcendentals=0),
        name="collect",
    )(*arrays)


def spread_kernel(counts, x_ref, *outs):
    length = x_ref.shape[0] // 2
    pieces = [(out, first) for out in outs for first in range(0, out.shape[2], length)]
    pair = 0
    for (out, first), count in zip(pieces, counts):
        cut = slice(first, first + length)
        for spot in range(0, count, 2):
            tile = x_ref[:, pair * LANES : (pair + 1) * LANES].astype(F32)
            packed = pack_pair(tile)
            for side in range(2):
                out[spot + side, 0, cut, :] = packed[side].astype(BF16)
            pair += 1
        for spot in range(count, out.shape[0]):
            out[spot, 0, cut, :] = jnp.zeros((length, LANES), BF16)


def spread(span, counts, micros, rows_array):
    rows, width = rows_array.shape
    half = rows // (2 * micros)
    lengths = [half // 2] + ([half // 2 * (len(counts) - 1)] if len(counts) > 1 else [])
    return pl.pallas_call(
        functools.partial(spread_kernel, counts),
        grid=(micros, 2),
        in_specs=[pl.BlockSpec((half, width), lambda m, i: (2 * m + i, 0))],
        out_specs=[
            pl.BlockSpec((span, 1, length, LANES), lambda m, i: (m, i, 0, 0)) for length in lengths
        ],
        out_shape=[
            jax.ShapeDtypeStruct((micros * span, 2, length, LANES), BF16) for length in lengths
        ],
        compiler_params=params(2),
        cost_estimate=pl.CostEstimate(flops=0, bytes_accessed=4 * 10**6, transcendentals=0),
        name="spread",
    )(rows_array)


def turn_back(tile, cos_table, sine_table):
    near = (lane_index(tile.shape[0]) % HEAD_DIM) < HEAD_DIM // 2
    scaled = tile * sine_table
    moved = jnp.where(
        near,
        pltpu.roll(scaled, LANES - HEAD_DIM // 2, 1),
        pltpu.roll(scaled, HEAD_DIM // 2, 1),
    )
    return tile * cos_table + moved


def collect_grad_kernel(count, c_ref, s_ref, in_ref, out):
    cos_table, sine_table = c_ref[...], s_ref[...]
    rows = cos_table.shape[0]
    span = count * HEAD_DIM
    low = lane_index(rows) < HEAD_DIM
    for pair in range(count // 2):
        kvs = [in_ref[2 * pair + side, 0, :rows, :].astype(F32) for side in range(2)]
        packed = [in_ref[2 * pair + side, 0, rows:, :].astype(F32) for side in range(2)]
        grad_k = jnp.where(low, kvs[0], flip(kvs[1]))
        grad_v = jnp.where(low, flip(kvs[0]), kvs[1])
        grad_q = turn_back(unpack_pair(*packed), cos_table, sine_table)
        grad_k = turn_back(grad_k, cos_table, sine_table)
        for part, value in enumerate((grad_q, grad_k, grad_v)):
            first = part * span + pair * LANES
            out[:, first : first + LANES] = value.astype(BF16)


def collect_grad(count, micros, array, cos_table, sine_table):
    units, _, depth, _ = array.shape
    half = depth * 2 // 3
    width = 3 * count * HEAD_DIM
    table = pl.BlockSpec((half, LANES), lambda m, i: (2 * m + i, 0))
    return pl.pallas_call(
        functools.partial(collect_grad_kernel, count),
        grid=(micros, 2),
        in_specs=[
            table,
            table,
            pl.BlockSpec((units // micros, 1, depth, LANES), lambda m, i: (m, i, 0, 0)),
        ],
        out_specs=pl.BlockSpec((half, width), lambda m, i: (2 * m + i, 0)),
        out_shape=jax.ShapeDtypeStruct((micros * 2 * half, width), BF16),
        compiler_params=params(2),
        cost_estimate=pl.CostEstimate(flops=0, bytes_accessed=6 * 10**6, transcendentals=0),
        name="collect_grad",
    )(cos_table, sine_table, array)


def matmul(left, right):
    return jnp.dot(left, right, preferred_element_type=F32)


def norm_backward(grad_out, values, recip_rows, gain):
    scaled = grad_out * gain
    grad_in = recip_rows * scaled - values * (recip_rows * recip_rows * recip_rows) * jnp.mean(
        scaled * values, -1, keepdims=True
    )
    return (grad_in, jnp.sum(grad_out * values * recip_rows, 0))


def feed_forward(tokens, cotangent, attended, w_out, gain_mlp, w_gate, w_up, w_down):
    inputs = tokens.astype(F32)
    gain = gain_mlp.astype(F32)
    middle = inputs + matmul(attended, w_out)
    recip = lax.rsqrt(jnp.mean(middle * middle, -1, keepdims=True) + EPS)
    mlp_low = (middle * recip * gain).astype(BF16)
    gate_pre = matmul(mlp_low, w_gate)
    up_pre = matmul(mlp_low, w_up)
    gate_sigmoid = jax.nn.sigmoid(gate_pre)
    silu_value = gate_pre * gate_sigmoid
    hidden_low = (silu_value * up_pre).astype(BF16)
    result = (middle + matmul(hidden_low, w_down)).astype(BF16)
    grad_hidden = jnp.einsum("td,fd->tf", cotangent, w_down, preferred_element_type=F32)
    grad_gate = (
        grad_hidden * up_pre * gate_sigmoid * (1.0 + gate_pre * (1.0 - gate_sigmoid))
    ).astype(BF16)
    grad_up = (grad_hidden * silu_value).astype(BF16)
    grad_normed = jnp.einsum(
        "tf,df->td", grad_gate, w_gate, preferred_element_type=F32
    ) + jnp.einsum("tf,df->td", grad_up, w_up, preferred_element_type=F32)
    grad_mid, grad_gain = norm_backward(grad_normed, middle, recip, gain)
    grad_middle = cotangent.astype(F32) + grad_mid
    grad_branch = grad_middle.astype(BF16)
    grad_att = jnp.einsum("te,de->td", grad_branch, w_out, preferred_element_type=F32).astype(BF16)
    return result, grad_middle, grad_att, grad_gain, (
        (attended, grad_branch),
        (mlp_low, grad_gate),
        (mlp_low, grad_up),
        (hidden_low, cotangent),
    )


def outer(left, right):
    return jnp.einsum("td,te->de", left, right, preferred_element_type=F32).astype(BF16)


def after(value, *others):
    return lax.optimization_barrier((value,) + others)[0]


def body(
    tokens, cotangent, doc_lengths, gain_attn, w_query, w_key, w_value, w_out, gain_mlp, w_gate, w_up, w_down
):
    micros, _, rows, width = tokens.shape
    heads = width // HEAD_DIM
    devices = lax.axis_size("ctx")
    shards = lax.axis_size("fsdp")
    place = lax.axis_index("ctx")
    side = lax.axis_index("fsdp")
    chips = devices // 2
    core = place % 2
    half = rows // 2
    depth = half + half // 2
    span = chips // micros
    rounds = -(-heads // span)
    counts = tuple(min(span, heads - index * span) for index in range(rounds))
    swap = [(i, i ^ 1) for i in range(devices)]
    cross = [(0, 1), (1, 0)]

    def pick(array, index, axis):
        return lax.dynamic_index_in_dim(array, index, axis, keepdims=False)

    def gathered(shard):
        return lax.all_gather(shard, "fsdp", axis=0, tiled=True)

    def fetched(shard):
        if shards != 2:
            return gathered(shard)
        depth_two = shard.reshape((2, shard.shape[0] // 2) + shard.shape[1:])
        near = lax.ppermute(pick(depth_two, core, 0), "fsdp", cross)
        far = lax.ppermute(near, "ctx", swap)
        away = jnp.where(core == 0, jnp.stack([near, far]), jnp.stack([far, near]))
        away = away.reshape(shard.shape)
        return jnp.where(
            side == 0, jnp.concatenate([shard, away]), jnp.concatenate([away, shard])
        )

    def fetched_line(line):
        if shards != 2:
            return gathered(line)
        away = lax.ppermute(line, "fsdp", cross)
        return jnp.where(side == 0, jnp.concatenate([line, away]), jnp.concatenate([away, line]))

    def columns(index):
        cut = slice(index * span * HEAD_DIM, (index * span + counts[index]) * HEAD_DIM)
        return jnp.concatenate([w_query[:, cut], w_key[:, cut], w_value[:, cut]], 1)

    gain_attn, gain_mlp = fetched_line(gain_attn), fetched_line(gain_mlp)
    in_weights = [fetched(columns(index)) for index in range(rounds)]
    w_out, w_gate, w_up, w_down = (gathered(shard) for shard in (w_out, w_gate, w_up, w_down))
    lengths = doc_lengths[:, 0]
    doc_ends = jnp.cumsum(lengths, -1)
    starts = (doc_ends - lengths).astype(jnp.int32)

    def begins_of(micro_starts, positions):
        reached = positions[:, None] >= micro_starts[None, :]
        return jnp.max(jnp.where(reached, micro_starts[None, :], 0), -1)

    lane = jnp.arange(LANES)
    inverse = jnp.power(10000.0, -(lane % (HEAD_DIM // 2)).astype(F32) / (HEAD_DIM // 2))
    sign = jnp.where((lane % HEAD_DIM) < HEAD_DIM // 2, -1.0, 1.0)
    positions = place * rows + jnp.arange(rows, dtype=jnp.int32)
    offsets = jnp.concatenate(
        [positions - begins_of(starts[micro], positions) for micro in range(micros)]
    ).astype(F32)
    angles = offsets[:, None] * inverse[None, :]
    cos_table, sine_table = jnp.cos(angles), jnp.sin(angles) * sign

    def exchange(buffer):
        return lax.all_to_all(buffer, "ctx", split_axis=0, concat_axis=0, tiled=True)

    tokens = tokens.reshape(micros * rows, width)
    cotangent = cotangent.reshape(micros * rows, width)
    inputs = tokens.astype(F32)
    recip = lax.rsqrt(jnp.mean(inputs * inputs, -1, keepdims=True) + EPS)
    normed = (inputs * recip * gain_attn.astype(F32)).astype(BF16)

    block = jnp.arange(devices, dtype=jnp.int32)
    block_first = block * rows + core * half
    chosen = pick(starts, place // 2 // span, 0)
    lowest = begins_of(chosen, block_first) // rows
    inner = jnp.minimum(-(-begins_of(chosen, block_first + half - 1) // rows), block)

    received, infos, others, attended_back, kept = [], [], [], [], []
    for index in range(rounds):
        live = index * span + place // 2 % span < heads
        bounds = jnp.stack([jnp.where(live, lowest, block), jnp.where(live, inner, block)], 1)
        infos.append(jnp.concatenate([core[None], bounds.reshape(-1)]).astype(jnp.int32))
        buffer = project(
            span, counts[index], micros, normed, cos_table, sine_table, in_weights[index]
        ).reshape(devices, depth, LANES)
        if index >= 2:
            buffer = after(buffer, kept[index - 2][1])
        received.append(exchange(buffer))
        whole = received[index]
        if index:
            whole = after(whole, kept[index - 1][1])
        others.append(lax.ppermute(whole, "ctx", swap))
        out, lse = attend(infos[index], chosen, received[index], others[index])
        kept.append((out, lse))
    def came_back(pieces):
        joined = pieces[0] if len(pieces) == 1 else jnp.concatenate(pieces, 1)
        joined = exchange(joined)
        return joined.reshape((chips, 2) + joined.shape[1:])

    early = [after(out, received[-1]) for out, _ in kept[:-1]]
    attended_back = ([came_back(early)] if early else []) + [came_back([kept[-1][0]])]

    attended = collect(counts, micros, attended_back)
    result, grad_middle, grad_att, grad_gain_mlp, pairs = feed_forward(
        tokens, cotangent, attended, w_out, gain_mlp, w_gate, w_up, w_down
    )
    grads_in = [
        exchange(buffer.reshape((devices,) + buffer.shape[2:]))
        for buffer in spread(span, counts, micros, grad_att)
    ]

    def paired(stay, leave, axis, routes):
        return (stay.astype(F32) + lax.ppermute(leave, axis, routes).astype(F32)).astype(BF16)

    def chip_summed(full, gain=None):
        count, wide = full.shape[0] // (2 * shards), full.shape[1]
        parts = full.reshape(shards, 2, count, wide)
        if gain is not None:
            line = gain.astype(BF16).reshape(shards, 2, 1, -1)
            line = jnp.pad(line, ((0, 0), (0, 0), (0, 15), (0, wide - line.shape[-1])))
            parts = jnp.concatenate([parts, line], 2)
        return paired(pick(parts, core, 1), pick(parts, 1 - core, 1), "ctx", swap)

    def owned(parts):
        if shards == 2:
            return paired(pick(parts, side, 0), pick(parts, 1 - side, 0), "fsdp", cross)
        return lax.psum_scatter(parts, "fsdp", scatter_dimension=0, tiled=False)

    alike = [list(range(first, devices, 2)) for first in range(2)]

    def totals_of(parts):
        totals = lax.psum(tuple(parts), "ctx", axis_index_groups=alike)
        found = []
        for total in totals:
            twin = lax.ppermute(total, "ctx", swap)
            found.append(jnp.where(core == 0, jnp.stack([total, twin]), jnp.stack([twin, total])))
        return found

    def opened(total, has_gain):
        wide = total.shape[-1]
        count = total.shape[1] - (16 if has_gain else 0)
        rows_part = total[:, :count].reshape(2 * count, wide).astype(F32)
        if not has_gain:
            return rows_part
        return rows_part, total[:, count, : width // (2 * shards)].reshape(-1).astype(F32)

    pair_out, pair_gate, pair_up, pair_down = pairs
    chip_down = chip_summed(outer(*pair_down))
    chip_gate = chip_summed(outer(*pair_gate))
    chip_up = chip_summed(outer(*pair_up))
    chip_out = chip_summed(outer(*pair_out), grad_gain_mlp)
    first_parts = [owned(chip_out), owned(chip_down)]
    second_parts = [owned(chip_gate), owned(chip_up)]
    first_totals = totals_of(first_parts)
    second_totals = totals_of([after(part, *first_totals) for part in second_parts])
    grad_w_out, grad_gain_mlp = opened(first_totals[0], True)
    grad_w_down = opened(first_totals[1], False)
    grad_w_gate, grad_w_up = (opened(total, False) for total in second_totals)

    grad_back = []
    waits = {0: (chip_out, chip_down, chip_gate, chip_up), 1: tuple(first_parts), 2: tuple(second_parts)}
    for index in range(rounds):
        own, away = attend_grad(
            infos[index],
            chosen,
            received[index],
            others[index],
            after(grads_in[min(index, 1)], *waits.get(index, ())),
            max(index - 1, 0),
            *kept[index],
        )
        back = lax.ppermute(away, "ctx", swap)
        own_kv = (own[:, :half].astype(F32) + back.astype(F32)).astype(BF16)
        buffer = jnp.concatenate([own_kv, own[:, half:]], 1)
        grad_back.append(exchange(buffer).reshape(chips, 2, depth, LANES))

    grad_normed, parts = 0.0, []
    for index in range(rounds):
        grad_qkv = collect_grad(counts[index], micros, grad_back[index], cos_table, sine_table)
        grad_normed = grad_normed + jnp.einsum(
            "te,de->td", grad_qkv, in_weights[index], preferred_element_type=F32
        )
        final = index == rounds - 1
        if final:
            grad_in, grad_gain = norm_backward(grad_normed, inputs, recip, gain_attn.astype(F32))
        parts.append(owned(chip_summed(outer(normed, grad_qkv), grad_gain if final else None)))
    last_totals = totals_of([after(part, *second_totals) for part in parts[:-1]]) if rounds > 1 else []
    last_totals = last_totals + totals_of([after(parts[-1], *second_totals, *last_totals)])
    grad_inputs = (grad_middle + grad_in).astype(BF16)
    opened_last, grad_gain_attn = opened(last_totals[-1], True)
    opened_parts = [opened(total, False) for total in last_totals[:-1]] + [opened_last]
    grad_w_query, grad_w_key, grad_w_value = (
        jnp.concatenate(
            [
                part[:, which * part.shape[1] // 3 : (which + 1) * part.shape[1] // 3]
                for part in opened_parts
            ],
            1,
        )
        for which in range(3)
    )
    shape = (micros, 1, rows, width)
    return (
        result.reshape(shape),
        grad_inputs.reshape(shape),
        grad_gain_attn,
        grad_w_query,
        grad_w_key,
        grad_w_value,
        grad_w_out,
        grad_gain_mlp,
        grad_w_gate,
        grad_w_up,
        grad_w_down,
    )


def solution(mesh):
    weight, gain = P("fsdp", None), P("fsdp")
    rows = P(None, "fsdp", "ctx", None)
    weights = (gain, weight, weight, weight, weight, gain, weight, weight, weight)
    return jax.shard_map(
        body,
        mesh=mesh,
        in_specs=(rows, rows, P(None, "fsdp", None)) + weights,
        out_specs=(rows, rows) + weights,
        check_vma=False,
    )
```

time: 978 us -> 845 us (0.86)
  waiting for transfers between devices: 384 us -> 253 us
  blocking collectives: 48.9 us -> 0 us
  other arithmetic: 37.6 us -> 81.5 us
  matrix products: 99 us -> 87.7 us
  Pallas kernels: 277 us -> 288 us
    all_to_all x12 -> x10, waiting for transfers between devices: 143 us -> 22.9 us  [exchange(): lax.all_to_all(buffer, 'ctx', split_axis=0, concat_axis=0, tiled=True)]
    psum x1 -> x3, waiting for transfers between devices: 100 us -> 199 us  [totals_of(): totals = lax.psum(tuple(parts), 'ctx', axis_index_groups=alike)]
    all_gather x7 -> x4, waiting for transfers between devices: 78 us -> 0.04 us  [gathered(): return lax.all_gather(shard, 'fsdp', axis=0, tiled=True)]
    reduce_scatter x7 -> x0, waiting for transfers between devices: 56.1 us -> none  [reduced(): lax.psum_scatter(full.astype(BF16), 'fsdp', scatter_dimension=0, tiled=True)]
    psum x1 -> x0, blocking collectives: 34 us -> none  [body(): totals = [lax.psum(part, 'ctx').astype(F32) for part in grads]]
    ppermute x3 -> x32, waiting for transfers between devices: 0.01 us -> 30.1 us  [the longest x14 10.4 us: paired(): lax.ppermute(leave, axis, routes).astype(F32)]
    all_to_all x12 -> x10, starting transfers between devices: 76.8 us -> 50.9 us  [exchange(): lax.all_to_all(buffer, 'ctx', split_axis=0, concat_axis=0, tiled=True)]
    convert_element_type x13 -> x27, other arithmetic: 12.7 us -> 38.3 us  [the longest x14 24.7 us: paired(): (stay.astype(F32) + lax.ppermute(leave, axis, routes).astype(F32)).astype...]
  transfers between devices with their start and end apart: 33 -> 52, of which waited for: 16 -> 13; matrix products, arithmetic and copies ran while one was open for 10% -> 19% of each run, Pallas kernels for 27% -> 34%
where the time goes in v2:
time: 845 us; the launch traced here: 829 us
  Pallas kernels  288 us (34%)
  waiting for transfers between devices  253 us (30%)
  matrix products  87.7 us (10%)
  other arithmetic  81.5 us (10%)
  starting transfers between devices  72.1 us (9%)
  local copies, waits for them, and re-layouts  31 us (4%)
  between operations  15.4 us (2%)
    psum x3, waiting for transfers between devices, totals_of(): totals = lax.psum(tuple(parts), 'ctx', axis_index_groups=alike)  199 us
    pallas_call x3, Pallas kernels, attend_grad(): pl.pallas_call(attend_grad_kernel, grid_spec=pltpu.PrefetchScalarGridSpec...  133 us
    pallas_call x3, Pallas kernels, attend(): pl.pallas_call(attend_kernel, grid_spec=pltpu.PrefetchScalarGridSpec(num_...  115 us
    all_to_all x10, starting transfers between devices, exchange(): lax.all_to_all(buffer, 'ctx', split_axis=0, concat_axis=0, tiled=True)  50.9 us
    dot_general x4, matrix products, matmul(): return jnp.dot(left, right, preferred_element_type=F32)  29.9 us
    dot_general x7, matrix products, outer(): jnp.einsum('td,te->de', left, right, preferred_element_type=F32)  25.3 us
    convert_element_type x14, other arithmetic, paired(): (stay.astype(F32) + lax.ppermute(leave, axis, routes).astype(F32)).astype...  24.7 us
    all_to_all x10, waiting for transfers between devices, exchange(): lax.all_to_all(buffer, 'ctx', split_axis=0, concat_axis=0, tiled=True)  22.9 us
  transfers between devices with their start and end apart: 52, of which 13 were waited for; matrix products, arithmetic and copies ran while one was open for 19% of the time, Pallas kernels for 34%

profile of v2, /device:TPU:0, one launch (start us, length us, event | category | flops | bytes accessed | tf_op | source)
XLA Modules:
  0.0 829.0 jit_solution(2848832319371262467)
XLA Ops:
  19.3 6.9 collective-permute-done
  30.7 7.8 maximum_select_fusion.3
  38.5 5.8 project.3
  44.3 6.2 all-to-all-start
  52.3 7.8 collective-permute-done.6
  61.7 20.8 %all-to-all-done.mine = bf16[16,384,128]{2,1,0:T(8,128)(2,1)} async-done(((bf16[16,384,128]{2,1,0:T(8,128)(2,1)}), bf16[16,384,128]{2,1,0:T(8,128)(2,1)}, u32[]{:S(2)}, u32[]{:S(2)}) %all-to-all-start) | async-done | bytes 1572896 | tf_op jit(solution)/shard_map/all_to_all | solution.py:540
  84.9 5.8 project.5
  90.7 8.5 %all-to-all-start.2 = ((bf16[16,384,128]{2,1,0:T(8,128)(2,1)}), bf16[16,384,128]{2,1,0:T(8,128)(2,1)S(1)}, u32[]{:S(2)}, u32[]{:S(2)}) async-start(bf16[16,384,128]{2,1,0:T(8,128)(2,1)} %bitcast.253), calls=%async_computation.2 | async-start | bytes 3145728 | tf_op jit(solution)/shard_map/all_to_all | solution.py:540
  100.3 38.2 %attend.3 = (bf16[16,128,128]{2,1,0:T(8,128)(2,1)}, f32[16,1,256]{2,1,0:T(1,128)}) custom-call(s32[33]{0:T(128)} %pad_add_fusion.3.info, s32[8]{0:T(128)} %copy-done.55, bf16[16,384,128]{2,1,0:T(8,128)(2,1)} %all-to-all-done.mine, bf16[16,384,128]{2,1,0:T(8,128)(2,1)} %collective-permute-done.3.other), custom_call_target="tpu_custom_call" | custom-call | flops 16000000000 | bytes 10000000 | tf_op jit(solution)/shard_map/attend/pallas_call | solution.py:175
  138.6 6.2 project.4
  150.8 38.3 %attend.4 = (bf16[16,128,128]{2,1,0:T(8,128)(2,1)}, f32[16,1,256]{2,1,0:T(1,128)}) custom-call(s32[33]{0:T(128)} %pad_add_fusion.4.info, s32[8]{0:T(128)} %copy-done.55, bf16[16,384,128]{2,1,0:T(8,128)(2,1)} %copy-done.31, bf16[16,384,128]{2,1,0:T(8,128)(2,1)} %collective-permute-done.8.other), custom_call_target="tpu_custom_call" | custom-call | flops 16000000000 | bytes 10000000 | tf_op jit(solution)/shard_map/attend/pallas_call | solution.py:175
  196.8 38.3 %attend.5 = (bf16[16,128,128]{2,1,0:T(8,128)(2,1)}, f32[16,1,256]{2,1,0:T(1,128)}) custom-call(s32[33]{0:T(128)} %pad_add_fusion.5.info, s32[8]{0:T(128)} %copy-done.55, bf16[16,384,128]{2,1,0:T(8,128)(2,1)} %all-to-all-done.1.mine, bf16[16,384,128]{2,1,0:T(8,128)(2,1)} %collective-permute-done.9.other), custom_call_target="tpu_custom_call" | custom-call | flops 16000000000 | bytes 10000000 | tf_op jit(solution)/shard_map/attend/pallas_call | solution.py:175
  243.2 9.2 %fusion.50 = f32[1024,2048]{1,0:T(8,128)} fusion(bf16[1024,768]{1,0:T(8,128)(2,1)} %bitcast.268, bf16[2048,768]{1,0:T(8,128)(2,1)} %all-gather.11.cloned.1.call-done), kind=kOutput, calls=%fused_computation.191 | convolution fusion | flops 3221225472 | bytes 13107200 | tf_op jit(solution)/shard_map/td,fd->tf/dot_general | solution.py:443
  263.6 7.5 fusion.49
  271.0 11.3 %multiply_convert_fusion = (bf16[1024,2048]{1,0:T(8,128)(2,1)S(1)}, bf16[1024,2048]{1,0:T(8,128)(2,1)S(1)}, bf16[1024,2048]{1,0:T(8,128)(2,1)S(1)}) fusion(f32[1024,2048]{1,0:T(8,128)} %fusion.50, f32[1024,2048]{1,0:T(8,128)} %fusion.49, bf16[1024,768]{1,0:T(8,128)(2,1)S(1)} %multiply_convert_fusion.3, bf16[768,2048]{1,0:T(8,128)(2,1)} %all-gather.7.cloned.1.call-done), kind=kOutput, calls=%fused_computation | convolution fusion | flops 3252682752 | bytes 34078720 | tf_op jit(solution)/shard_map/dot_general | solution.py:420
  351.3 44.2 %attend_grad.3 = (bf16[16,384,128]{2,1,0:T(8,128)(2,1)}, bf16[16,256,128]{2,1,0:T(8,128)(2,1)}) custom-call(s32[33]{0:T(128)} %pad_add_fusion.3.info, s32[8]{0:T(128)} %copy-done.55, bf16[16,384,128]{2,1,0:T(8,128)(2,1)} %all-to-all-done.mine, bf16[16,384,128]{2,1,0:T(8,128)(2,1)} %collective-permute-done.3.other, ...), custom_call_target="tpu_custom_call" | custom-call | flops 32000000000 | bytes 10000000 | tf_op jit(solution)/shard_map/attend_grad/pallas_call | solution.py:272
  413.3 44.2 %attend_grad.4 = (bf16[16,384,128]{2,1,0:T(8,128)(2,1)}, bf16[16,256,128]{2,1,0:T(8,128)(2,1)}) custom-call(s32[33]{0:T(128)} %pad_add_fusion.4.info, s32[8]{0:T(128)} %copy-done.55, bf16[16,384,128]{2,1,0:T(8,128)(2,1)} %copy-done.31, bf16[16,384,128]{2,1,0:T(8,128)(2,1)} %collective-permute-done.8.other, bf16[16,256,128]{2,1,0:T(8,128)(2,1)} %all-to-all-done.7.do_ref, ...), custom_call_target="tpu_custom_call" | custom-call | flops 32000000000 | bytes 10000000 | tf_op jit(solution)/shard_map/attend_grad/pallas_call | solution.py:272
  471.3 44.2 %attend_grad.5 = (bf16[16,384,128]{2,1,0:T(8,128)(2,1)}, bf16[16,256,128]{2,1,0:T(8,128)(2,1)}) custom-call(s32[33]{0:T(128)} %pad_add_fusion.5.info, s32[8]{0:T(128)} %copy-done.55, bf16[16,384,128]{2,1,0:T(8,128)(2,1)} %all-to-all-done.1.mine, bf16[16,384,128]{2,1,0:T(8,128)(2,1)} %collective-permute-done.9.other, ...), custom_call_target="tpu_custom_call" | custom-call | flops 32000000000 | bytes 10000000 | tf_op jit(solution)/shard_map/attend_grad/pallas_call | solution.py:272
  515.6 38.0 %all-reduce.13.cloned.1.call-done = (bf16[208,768]{1,0:T(8,128)(2,1)}, bf16[512,768]{1,0:T(8,128)(2,1)}) async-done(((bf16[208,768]{1,0:T(8,128)(2,1)}, bf16[512,768]{1,0:T(8,128)(2,1)}), (bf16[208,768]{1,0:T(8,128)(2,1)}, bf16[512,768]{1,0:T(8,128)(2,1)})) %all-reduce.13.cloned.1.call-update) | async-done | bytes 1105936 | tf_op jit(solution)/shard_map/psum | solution.py:608
  553.6 7.8 add_convert_fusion
  590.0 92.4 %all-reduce.11.cloned.1.call-done = (bf16[192,2048]{1,0:T(8,128)(2,1)}, bf16[192,2048]{1,0:T(8,128)(2,1)}) async-done(((bf16[192,2048]{1,0:T(8,128)(2,1)}, bf16[192,2048]{1,0:T(8,128)(2,1)}), (bf16[192,2048]{1,0:T(8,128)(2,1)}, bf16[192,2048]{1,0:T(8,128)(2,1)})) %all-reduce.11.cloned.1.call-update) | async-done | bytes 1572880 | tf_op jit(solution)/shard_map/psum | solution.py:608
  710.6 5.5 fusion.13
  731.8 5.6 collective-permute-done.23
  744.6 68.6 %all-reduce.9.cloned.1.call-done = (bf16[208,768]{1,0:T(8,128)(2,1)}, bf16[192,768]{1,0:T(8,128)(2,1)}, bf16[192,768]{1,0:T(8,128)(2,1)}) async-done(((bf16[208,768]{1,0:T(8,128)(2,1)}, bf16[192,768]{1,0:T(8,128)(2,1)}, bf16[192,768]{1,0:T(8,128)(2,1)}), (bf16[208,768]{1,0:T(8,128)(2,1)}, bf16[192,768]{1,0:T(8,128)(2,1)}, bf16[192,768]{1,0:T(8,128)(2,1)})) %all-reduce.9.cloned.1.call-update) | async-done | bytes 909328 | tf_op jit(solution)/shard_map/psum | solution.py:608
  (364 shorter events, 244.1 us)
Async XLA Ops:
  44.3 38.2 %all-to-all-start = ((bf16[16,384,128]{2,1,0:T(8,128)(2,1)}), bf16[16,384,128]{2,1,0:T(8,128)(2,1)}, u32[]{:S(2)}, u32[]{:S(2)}) async-start(bf16[16,384,128]{2,1,0:T(8,128)(2,1)} %bitcast.254), calls=%async_computation | async-start | bytes 3145728 | tf_op jit(solution)/shard_map/all_to_all | solution.py:540
  50.6 192.6 %all-gather.11.cloned.1.call-start = ((), (), s32[]{:S(2)}) async-start(), calls=%async_computation.13 | async-start | bytes 4718592 | tf_op jit(solution)/shard_map/all_gather | solution.py:494
  90.7 47.8 %all-to-all-start.2 = ((bf16[16,384,128]{2,1,0:T(8,128)(2,1)}), bf16[16,384,128]{2,1,0:T(8,128)(2,1)S(1)}, u32[]{:S(2)}, u32[]{:S(2)}) async-start(bf16[16,384,128]{2,1,0:T(8,128)(2,1)} %bitcast.253), calls=%async_computation.2 | async-start | bytes 3145728 | tf_op jit(solution)/shard_map/all_to_all | solution.py:540
  99.2 159.0 %all-gather.5.cloned.1.call-start = ((), (), s32[]{:S(2)}) async-start(), calls=%async_computation.10 | async-start | bytes 1769472 | tf_op jit(solution)/shard_map/all_gather | solution.py:494
  144.9 44.3 %all-to-all-start.1 = ((bf16[16,384,128]{2,1,0:T(8,128)(2,1)}), bf16[16,384,128]{2,1,0:T(8,128)(2,1)}, u32[]{:S(2)}, u32[]{:S(2)}) async-start(bf16[16,384,128]{2,1,0:T(8,128)(2,1)} %bitcast.255), calls=%async_computation.1 | async-start | bytes 3145728 | tf_op jit(solution)/shard_map/all_to_all | solution.py:540
  149.3 114.3 %all-gather.9.cloned.1.call-start = ((), (), s32[]{:S(2)}) async-start(), calls=%async_computation.12 | async-start | bytes 4718592 | tf_op jit(solution)/shard_map/all_gather | solution.py:494
  191.2 43.9 %all-to-all-start.3 = ((bf16[16,256,128]{2,1,0:T(8,128)(2,1)}), bf16[16,256,128]{2,1,0:T(8,128)(2,1)S(1)}, u32[]{:S(2)}, u32[]{:S(2)}) async-start(bf16[16,256,128]{2,1,0:T(8,128)(2,1)} %pad_maximum_fusion.6), calls=%async_computation.3 | async-start | bytes 2097152 | tf_op jit(solution)/shard_map/all_to_all | solution.py:540
  195.4 75.6 %all-gather.7.cloned.1.call-start = ((), (), s32[]{:S(2)}) async-start(), calls=%async_computation.11 | async-start | bytes 4718592 | tf_op jit(solution)/shard_map/all_gather | solution.py:494
  288.4 45.7 %collective-permute-start.12 = (bf16[2,512,768]{2,1,0:T(8,128)(2,1)}, bf16[2,512,768]{2,1,0:T(8,128)(2,1)}, u32[]{:S(2)}, u32[]{:S(2)}) collective-permute-start(bf16[2,512,768]{2,1,0:T(8,128)(2,1)} %dynamic-slice_bitcast_fusion.2), channel_id=1, source_target_pairs={{0,2},{2,0},{4,6},{6,4},{8,10},{10,8},{12,14},{14,12},{16,18},{18,... | collective-permute-start | bytes 4718600 | tf_op jit(solution)/shard_map/ppermute | solution.py:589
  333.0 62.5 %collective-permute-start.16 = (bf16[208,768]{1,0:T(8,128)(2,1)}, bf16[208,768]{1,0:T(8,128)(2,1)S(1)}, u32[]{:S(2)}, u32[]{:S(2)}) collective-permute-start(bf16[208,768]{1,0:T(8,128)(2,1)} %dynamic-slice_bitcast_fusion.11), channel_id=1, source_target_pairs={{0,1},{1,0},{2,3},{3,2},{4,5},{5,4},{6,7},{7,6},{8,9},{9,8},{10,11... | collective-permute-start | bytes 958472 | tf_op jit(solution)/shard_map/ppermute | solution.py:589
  345.0 60.7 %all-to-all-start.7 = ((bf16[16,256,128]{2,1,0:T(8,128)(2,1)}), bf16[16,256,128]{2,1,0:T(8,128)(2,1)}, u32[]{:S(2)}, u32[]{:S(2)}) async-start(bf16[16,256,128]{2,1,0:T(8,128)(2,1)} %bitcast.279), calls=%async_computation.7 | async-start | bytes 2097152 | tf_op jit(solution)/shard_map/all_to_all | solution.py:540
  350.4 53.0 %collective-permute-start.17 = (bf16[512,768]{1,0:T(8,128)(2,1)}, bf16[512,768]{1,0:T(8,128)(2,1)}, u32[]{:S(2)}, u32[]{:S(2)}) collective-permute-start(bf16[512,768]{1,0:T(8,128)(2,1)} %dynamic-slice_bitcast_fusion.5), channel_id=1, source_target_pairs={{0,1},{1,0},{2,3},{3,2},{4,5},{5,4},{6,7},{7,6},{8,9},{9,8},{10,11... | collective-permute-start | bytes 2359304 | tf_op jit(solution)/shard_map/ppermute | solution.py:589
  400.4 57.1 %collective-permute-start.20 = (bf16[192,2048]{1,0:T(8,128)(2,1)}, bf16[192,2048]{1,0:T(8,128)(2,1)}, u32[]{:S(2)}, u32[]{:S(2)}) collective-permute-start(bf16[192,2048]{1,0:T(8,128)(2,1)} %dynamic-slice_bitcast_fusion.3), channel_id=1, source_target_pairs={{0,1},{1,0},{2,3},{3,2},{4,5},{5,4},{6,7},{7,6},{8,9},{9,8},{10,11... | collective-permute-start | bytes 2359304 | tf_op jit(solution)/shard_map/ppermute | solution.py:589
  402.3 57.9 %collective-permute-start.19 = (bf16[192,2048]{1,0:T(8,128)(2,1)}, bf16[192,2048]{1,0:T(8,128)(2,1)}, u32[]{:S(2)}, u32[]{:S(2)}) collective-permute-start(bf16[192,2048]{1,0:T(8,128)(2,1)} %dynamic-slice_bitcast_fusion.4), channel_id=1, source_target_pairs={{0,1},{1,0},{2,3},{3,2},{4,5},{5,4},{6,7},{7,6},{8,9},{9,8},{10,11... | collective-permute-start | bytes 2359304 | tf_op jit(solution)/shard_map/ppermute | solution.py:589
  408.8 57.8 %all-to-all-start.6 = ((bf16[16,384,128]{2,1,0:T(8,128)(2,1)}), bf16[16,384,128]{2,1,0:T(8,128)(2,1)}, u32[]{:S(2)}, u32[]{:S(2)}) async-start(bf16[16,384,128]{2,1,0:T(8,128)(2,1)} %pad_maximum_fusion), calls=%async_computation.6 | async-start | bytes 3145728 | tf_op jit(solution)/shard_map/all_to_all | solution.py:540
  413.3 140.3 %all-reduce.13.cloned.1.call-start = ((), (), s32[]{:S(2)}) async-start(), calls=%async_computation.16 | async-start | bytes 2211840 | tf_op jit(solution)/shard_map/psum | solution.py:608
  466.7 98.2 %all-to-all-start.8 = ((bf16[16,384,128]{2,1,0:T(8,128)(2,1)}), bf16[16,384,128]{2,1,0:T(8,128)(2,1)}, u32[]{:S(2)}, u32[]{:S(2)}) async-start(bf16[16,384,128]{2,1,0:T(8,128)(2,1)} %pad_maximum_fusion.1), calls=%async_computation.8 | async-start | bytes 3145728 | tf_op jit(solution)/shard_map/all_to_all | solution.py:540
  515.6 46.4 %collective-permute-start.21 = (bf16[16,256,128]{2,1,0:T(8,128)(2,1)}, bf16[16,256,128]{2,1,0:T(8,128)(2,1)}, u32[]{:S(2)}, u32[]{:S(2)}) collective-permute-start(bf16[16,256,128]{2,1,0:T(8,128)(2,1)} %get-tuple-element.59), channel_id=1, source_target_pairs={{0,2},{2,0},{4,6},{6,4},{8,10},{10,8},{12,14},{14,12},{16,18},{18,... | collective-permute-start | bytes 3145736 | tf_op jit(solution)/shard_map/ppermute | solution.py:648
  564.9 135.4 %all-to-all-start.9 = ((bf16[16,384,128]{2,1,0:T(8,128)(2,1)}), bf16[16,384,128]{2,1,0:T(8,128)(2,1)S(1)}, u32[]{:S(2)}, u32[]{:S(2)}) async-start(bf16[16,384,128]{2,1,0:T(8,128)(2,1)} %pad_maximum_fusion.2), calls=%async_computation.9 | async-start | bytes 3145728 | tf_op jit(solution)/shard_map/all_to_all | solution.py:540
  568.8 113.6 %all-reduce.11.cloned.1.call-start = ((), (), s32[]{:S(2)}) async-start(), calls=%async_computation.15 | async-start | bytes 3145728 | tf_op jit(solution)/shard_map/psum | solution.py:608
  572.4 240.9 %all-reduce.9.cloned.1.call-start = ((), (), s32[]{:S(2)}) async-start(), calls=%async_computation.14 | async-start | bytes 1818624 | tf_op jit(solution)/shard_map/psum | solution.py:608
  584.5 98.4 %collective-permute-start.29 = (bf16[2,192,768]{2,1,0:T(8,128)(2,1)}, bf16[2,192,768]{2,1,0:T(8,128)(2,1)}, u32[]{:S(2)}, u32[]{:S(2)}) collective-permute-start(bf16[2,192,768]{2,1,0:T(8,128)(2,1)} %dynamic-slice_bitcast_fusion.9), channel_id=1, source_target_pairs={{0,2},{2,0},{4,6},{6,4},{8,10},{10,8},{12,14},{14,12},{16,18},{18,... | collective-permute-start | bytes 1769480 | tf_op jit(solution)/shard_map/ppermute | solution.py:589
  682.4 35.7 %collective-permute-start.27 = (bf16[192,2048]{1,0:T(8,128)(2,1)}, bf16[192,2048]{1,0:T(8,128)(2,1)}, u32[]{:S(2)}, u32[]{:S(2)}) collective-permute-start(bf16[192,2048]{1,0:T(8,128)(2,1)} %get-tuple-element.110), channel_id=1, source_target_pairs={{0,2},{2,0},{4,6},{6,4},{8,10},{10,8},{12,14},{14,12},{16,18},{18,... | collective-permute-start | bytes 2359304 | tf_op jit(solution)/shard_map/ppermute | solution.py:611
  682.4 41.1 %collective-permute-start.26 = (bf16[192,2048]{1,0:T(8,128)(2,1)}, bf16[192,2048]{1,0:T(8,128)(2,1)}, u32[]{:S(2)}, u32[]{:S(2)}) collective-permute-start(bf16[192,2048]{1,0:T(8,128)(2,1)} %get-tuple-element.109), channel_id=1, source_target_pairs={{0,2},{2,0},{4,6},{6,4},{8,10},{10,8},{12,14},{14,12},{16,18},{18,... | collective-permute-start | bytes 2359304 | tf_op jit(solution)/shard_map/ppermute | solution.py:611
  (90 other events, 827.6 us)
Sparse Core Ops, SparseCore 0:
  60.2 46.0 all-gather.10
  138.7 22.2 all-gather.4
  162.6 44.9 all-gather.8
  209.0 44.9 all-gather.6
  457.6 95.8 all-reduce.12
  572.9 109.4 all-reduce.10
  738.4 74.8 all-reduce.8

commit v3 on v2

--- a/solution.py
+++ b/solution.py
@@ -70,7 +70,23 @@
     )
 
 
-def project_kernel(count, n_ref, c_ref, s_ref, w_ref, out):
+def project_kernel(count, info, n_ref, c_ref, s_ref, *refs):
+    *parts, out, w_ref = refs
+
+    @pl.when((pl.program_id(0) == 0) & (pl.program_id(1) == 0))
+    def _():
+        if len(parts) == 1:
+            w_ref[...] = parts[0][...]
+            return
+        own, near, far = parts
+        deep, wide = near.shape
+        side, core = info[0], info[1]
+        mine = pl.ds(pl.multiple_of(side * deep, deep), deep)
+        away = pl.ds(pl.multiple_of((1 - side) * deep, deep), deep)
+        w_ref[mine, :] = own[...]
+        w_ref[away, pl.ds(pl.multiple_of(core * wide, wide), wide)] = near[...]
+        w_ref[away, pl.ds(pl.multiple_of((1 - core) * wide, wide), wide)] = far[...]
+
     joined = dot_nn(n_ref[...], w_ref[...])
     cos_table, sine_table = c_ref[...], s_ref[...]
     rows = n_ref.shape[0]
@@ -90,27 +106,37 @@
         out[count:] = jnp.zeros((out.shape[0] - count,) + out.shape[1:], BF16)
 
 
-def project(span, count, micros, normed, cos_table, sine_table, weight):
+def project(span, count, micros, info, normed, cos_table, sine_table, parts):
     rows, width = normed.shape
     half = rows // (2 * micros)
     depth = half + half // 2
+    wide = parts[0].shape[1]
     return pl.pallas_call(
         functools.partial(project_kernel, count),
-        grid=(micros, 2),
-        in_specs=[
-            pl.BlockSpec((half, width), lambda m, i: (2 * m + i, 0)),
-            pl.BlockSpec((half, LANES), lambda m, i: (2 * m + i, 0)),
-            pl.BlockSpec((half, LANES), lambda m, i: (2 * m + i, 0)),
-            full_block(weight.shape),
+        grid_spec=pltpu.PrefetchScalarGridSpec(
+            num_scalar_prefetch=1,
+            grid=(micros, 2),
+            in_specs=[
+                pl.BlockSpec((half, width), lambda m, i, *_: (2 * m + i, 0)),
+                pl.BlockSpec((half, LANES), lambda m, i, *_: (2 * m + i, 0)),
+                pl.BlockSpec((half, LANES), lambda m, i, *_: (2 * m + i, 0)),
+            ]
+            + [full_block(part.shape) for part in parts],
+            out_specs=[
+                pl.BlockSpec((span, 1, depth, LANES), lambda m, i, *_: (m, i, 0, 0)),
+                full_block((width, wide)),
+            ],
+        ),
+        out_shape=[
+            jax.ShapeDtypeStruct((micros * span, 2, depth, LANES), BF16),
+            jax.ShapeDtypeStruct((width, wide), BF16),
         ],
-        out_specs=pl.BlockSpec((span, 1, depth, LANES), lambda m, i: (m, i, 0, 0)),
-        out_shape=jax.ShapeDtypeStruct((micros * span, 2, depth, LANES), BF16),
         compiler_params=params(2),
         cost_estimate=pl.CostEstimate(
-            flops=2 * rows * width * weight.shape[1], bytes_accessed=4 * rows * width, transcendentals=0
+            flops=2 * rows * width * wide, bytes_accessed=4 * rows * width, transcendentals=0
         ),
         name="project",
-    )(normed, cos_table, sine_table, weight)
+    )(info, normed, cos_table, sine_table, *parts)
 
 
 def row_begins(starts_ref, positions):
@@ -495,28 +521,28 @@
 
     def fetched(shard):
         if shards != 2:
-            return gathered(shard)
-        depth_two = shard.reshape((2, shard.shape[0] // 2) + shard.shape[1:])
-        near = lax.ppermute(pick(depth_two, core, 0), "fsdp", cross)
-        far = lax.ppermute(near, "ctx", swap)
-        away = jnp.where(core == 0, jnp.stack([near, far]), jnp.stack([far, near]))
-        away = away.reshape(shard.shape)
+            return [gathered(shard)]
+        wide = shard.shape[1] // 2
+        near = lax.dynamic_slice_in_dim(shard, core * wide, wide, 1)
+        near = lax.ppermute(near, "fsdp", cross)
+        return [shard, near, lax.ppermute(near, "ctx", swap)]
+
+    def fetched_lines(lines):
+        if shards != 2:
+            return [gathered(line) for line in lines]
+        lines = jnp.stack(lines)
+        away = lax.ppermute(lines, "fsdp", cross)
         return jnp.where(
-            side == 0, jnp.concatenate([shard, away]), jnp.concatenate([away, shard])
+            side == 0, jnp.concatenate([lines, away], 1), jnp.concatenate([away, lines], 1)
         )
-
-    def fetched_line(line):
-        if shards != 2:
-            return gathered(line)
-        away = lax.ppermute(line, "fsdp", cross)
-        return jnp.where(side == 0, jnp.concatenate([line, away]), jnp.concatenate([away, line]))
 
     def columns(index):
         cut = slice(index * span * HEAD_DIM, (index * span + counts[index]) * HEAD_DIM)
         return jnp.concatenate([w_query[:, cut], w_key[:, cut], w_value[:, cut]], 1)
 
-    gain_attn, gain_mlp = fetched_line(gain_attn), fetched_line(gain_mlp)
-    in_weights = [fetched(columns(index)) for index in range(rounds)]
+    gain_attn, gain_mlp = fetched_lines([gain_attn, gain_mlp])
+    weight_parts = [fetched(columns(index)) for index in range(rounds)]
+    spot = jnp.stack([side, core]).astype(jnp.int32)
     w_out, w_gate, w_up, w_down = (gathered(shard) for shard in (w_out, w_gate, w_up, w_down))
     lengths = doc_lengths[:, 0]
     doc_ends = jnp.cumsum(lengths, -1)
@@ -551,14 +577,16 @@
     lowest = begins_of(chosen, block_first) // rows
     inner = jnp.minimum(-(-begins_of(chosen, block_first + half - 1) // rows), block)
 
-    received, infos, others, attended_back, kept = [], [], [], [], []
+    received, infos, others, attended_back, kept, in_weights = [], [], [], [], [], []
     for index in range(rounds):
         live = index * span + place // 2 % span < heads
         bounds = jnp.stack([jnp.where(live, lowest, block), jnp.where(live, inner, block)], 1)
         infos.append(jnp.concatenate([core[None], bounds.reshape(-1)]).astype(jnp.int32))
-        buffer = project(
-            span, counts[index], micros, normed, cos_table, sine_table, in_weights[index]
-        ).reshape(devices, depth, LANES)
+        buffer, weight = project(
+            span, counts[index], micros, spot, normed, cos_table, sine_table, weight_parts[index]
+        )
+        in_weights.append(weight)
+        buffer = buffer.reshape(devices, depth, LANES)
         if index >= 2:
             buffer = after(buffer, kept[index - 2][1])
         received.append(exchange(buffer))
@@ -602,15 +630,11 @@
             return paired(pick(parts, side, 0), pick(parts, 1 - side, 0), "fsdp", cross)
         return lax.psum_scatter(parts, "fsdp", scatter_dimension=0, tiled=False)
 
-    alike = [list(range(first, devices, 2)) for first in range(2)]
+    def spaced(part):
+        return jnp.where((core == jnp.arange(2))[:, None, None], part[None], 0)
 
     def totals_of(parts):
-        totals = lax.psum(tuple(parts), "ctx", axis_index_groups=alike)
-        found = []
-        for total in totals:
-            twin = lax.ppermute(total, "ctx", swap)
-            found.append(jnp.where(core == 0, jnp.stack([total, twin]), jnp.stack([twin, total])))
-        return found
+        return list(lax.psum(tuple(parts), "ctx"))
 
     def opened(total, has_gain):
         wide = total.shape[-1]
@@ -625,31 +649,35 @@
     chip_gate = chip_summed(outer(*pair_gate))
     chip_up = chip_summed(outer(*pair_up))
     chip_out = chip_summed(outer(*pair_out), grad_gain_mlp)
-    first_parts = [owned(chip_out), owned(chip_down)]
-    second_parts = [owned(chip_gate), owned(chip_up)]
+    first_parts = [spaced(owned(chip_out)), spaced(owned(chip_down))]
+    second_parts = [spaced(owned(chip_gate)), spaced(owned(chip_up))]
     first_totals = totals_of(first_parts)
     second_totals = totals_of([after(part, *first_totals) for part in second_parts])
     grad_w_out, grad_gain_mlp = opened(first_totals[0], True)
     grad_w_down = opened(first_totals[1], False)
     grad_w_gate, grad_w_up = (opened(total, False) for total in second_totals)
 
-    grad_back = []
-    waits = {0: (chip_out, chip_down, chip_gate, chip_up), 1: tuple(first_parts), 2: tuple(second_parts)}
+    grad_back, sent_back = [], []
+    waits = {0: (chip_out, chip_down, chip_gate, chip_up), 1: tuple(first_parts), 2: (*second_parts, *first_totals)}
     for index in range(rounds):
         own, away = attend_grad(
             infos[index],
             chosen,
             received[index],
             others[index],
-            after(grads_in[min(index, 1)], *waits.get(index, ())),
+            after(
+                grads_in[min(index, 1)], *waits.get(index, ()), *sent_back[-1:], *grad_back[-2:-1]
+            ),
             max(index - 1, 0),
             *kept[index],
         )
         back = lax.ppermute(away, "ctx", swap)
         own_kv = (own[:, :half].astype(F32) + back.astype(F32)).astype(BF16)
         buffer = jnp.concatenate([own_kv, own[:, half:]], 1)
+        sent_back.append(buffer)
         grad_back.append(exchange(buffer).reshape(chips, 2, depth, LANES))
 
+    grad_back[0] = after(grad_back[0], *second_totals)
     grad_normed, parts = 0.0, []
     for index in range(rounds):
         grad_qkv = collect_grad(counts[index], micros, grad_back[index], cos_table, sine_table)
@@ -659,9 +687,11 @@
         final = index == rounds - 1
         if final:
             grad_in, grad_gain = norm_backward(grad_normed, inputs, recip, gain_attn.astype(F32))
-        parts.append(owned(chip_summed(outer(normed, grad_qkv), grad_gain if final else None)))
-    last_totals = totals_of([after(part, *second_totals) for part in parts[:-1]]) if rounds > 1 else []
-    last_totals = last_totals + totals_of([after(parts[-1], *second_totals, *last_totals)])
+        parts.append(
+            spaced(owned(chip_summed(outer(normed, grad_qkv), grad_gain if final else None)))
+        )
+    last_totals = totals_of(parts[:-1]) if rounds > 1 else []
+    last_totals = last_totals + totals_of([after(parts[-1], *last_totals)])
     grad_inputs = (grad_middle + grad_in).astype(BF16)
     opened_last, grad_gain_attn = opened(last_totals[-1], True)
     opened_parts = [opened(total, False) for total in last_totals[:-1]] + [opened_last]

time: 845 us -> 991 us (1.17)
  waiting for transfers between devices: 253 us -> 411 us
  other arithmetic: 81.5 us -> 63.7 us
    psum x3 -> x4, waiting for transfers between devices: 199 us -> 330 us  [totals_of(): return list(lax.psum(tuple(parts), 'ctx'))]
    ppermute x14, waiting for transfers between devices: 10.4 us -> 31.6 us  [paired(): lax.ppermute(leave, axis, routes).astype(F32)]
    select_n x12 -> x6, other arithmetic: 20.1 us -> 7.08 us  [the longest x5 6.32 us: spaced(): return jnp.where((core == jnp.arange(2))[:, None, None], part[None], 0)]
    all_to_all x10, starting transfers between devices: 50.9 us -> 62.9 us  [exchange(): lax.all_to_all(buffer, 'ctx', split_axis=0, concat_axis=0, tiled=True)]
    ppermute x15 -> x7, waiting for transfers between devices: 19.7 us -> 20.6 us  [the longest x3 20.3 us: fetched(): near = lax.ppermute(near, 'fsdp', cross)]
  transfers between devices with their start and end apart: 52 -> 45, of which waited for: 13 -> 15; matrix products, arithmetic and copies ran while one was open for 19% -> 16% of each run, Pallas kernels for 34% -> 28%
where the time goes in v3:
time: 991 us; the launch traced here: 983 us
  waiting for transfers between devices  411 us (41%)
  Pallas kernels  285 us (29%)
  matrix products  90.7 us (9%)
  starting transfers between devices  76.1 us (8%)
  other arithmetic  63.7 us (6%)
  local copies, waits for them, and re-layouts  39.9 us (4%)
  between operations  15.7 us (2%)
    psum x4, waiting for transfers between devices, totals_of(): return list(lax.psum(tuple(parts), 'ctx'))  330 us
    pallas_call x3, Pallas kernels, attend_grad(): pl.pallas_call(attend_grad_kernel, grid_spec=pltpu.PrefetchScalarGridSpec...  129 us
    pallas_call x3, Pallas kernels, attend(): pl.pallas_call(attend_kernel, grid_spec=pltpu.PrefetchScalarGridSpec(num_...  112 us
    all_to_all x10, starting transfers between devices, exchange(): lax.all_to_all(buffer, 'ctx', split_axis=0, concat_axis=0, tiled=True)  62.9 us
    ppermute x14, waiting for transfers between devices, paired(): lax.ppermute(leave, axis, routes).astype(F32)  31.6 us
    dot_general x4, matrix products, matmul(): return jnp.dot(left, right, preferred_element_type=F32)  29.9 us
    all_to_all x10, waiting for transfers between devices, exchange(): lax.all_to_all(buffer, 'ctx', split_axis=0, concat_axis=0, tiled=True)  26.9 us
    dot_general x7, matrix products, outer(): jnp.einsum('td,te->de', left, right, preferred_element_type=F32)  25.6 us
  transfers between devices with their start and end apart: 45, of which 15 were waited for; matrix products, arithmetic and copies ran while one was open for 16% of the time, Pallas kernels for 28%

profile of v3, /device:TPU:0, one launch (start us, length us, event | category | flops | bytes accessed | tf_op | source)
XLA Modules:
  0.0 982.8 jit_solution(9775732935065378364)
XLA Ops:
  26.6 7.0 project.3
  40.4 8.7 collective-permute-done.6.refs_1_
  49.1 22.4 %all-to-all-done.mine = bf16[16,384,128]{2,1,0:T(8,128)(2,1)} async-done(((bf16[16,384,128]{2,1,0:T(8,128)(2,1)}), bf16[16,384,128]{2,1,0:T(8,128)(2,1)}, u32[]{:S(2)}, u32[]{:S(2)}) %all-to-all-start) | async-done | bytes 1572896 | tf_op jit(solution)/shard_map/all_to_all | solution.py:566
  73.2 7.0 project.5
  80.2 8.5 all-to-all-start.2
  92.2 8.4 collective-permute-done.4.refs_1_
  100.6 37.2 %attend.3 = (bf16[16,128,128]{2,1,0:T(8,128)(2,1)}, f32[16,1,256]{2,1,0:T(1,128)}) custom-call(s32[33]{0:T(128)} %pad_add_fusion.3.info, s32[8]{0:T(128)} %copy-done.54, bf16[16,384,128]{2,1,0:T(8,128)(2,1)} %all-to-all-done.mine, bf16[16,384,128]{2,1,0:T(8,128)(2,1)} %collective-permute-done.3.other), custom_call_target="tpu_custom_call" | custom-call | flops 16000000000 | bytes 10000000 | tf_op jit(solution)/shard_map/attend/pallas_call | solution.py:201
  138.8 7.0 project.4
  153.8 37.4 %attend.4 = (bf16[16,128,128]{2,1,0:T(8,128)(2,1)}, f32[16,1,256]{2,1,0:T(1,128)}) custom-call(s32[33]{0:T(128)} %pad_add_fusion.5.info, s32[8]{0:T(128)} %copy-done.54, bf16[16,384,128]{2,1,0:T(8,128)(2,1)} %copy-done.29, bf16[16,384,128]{2,1,0:T(8,128)(2,1)} %collective-permute-done.8.other), custom_call_target="tpu_custom_call" | custom-call | flops 16000000000 | bytes 10000000 | tf_op jit(solution)/shard_map/attend/pallas_call | solution.py:201
  201.6 37.2 %attend.5 = (bf16[16,128,128]{2,1,0:T(8,128)(2,1)}, f32[16,1,256]{2,1,0:T(1,128)}) custom-call(s32[33]{0:T(128)} %pad_add_fusion.6.info, s32[8]{0:T(128)} %copy-done.54, bf16[16,384,128]{2,1,0:T(8,128)(2,1)} %all-to-all-done.1.mine, bf16[16,384,128]{2,1,0:T(8,128)(2,1)} %collective-permute-done.9.other), custom_call_target="tpu_custom_call" | custom-call | flops 16000000000 | bytes 10000000 | tf_op jit(solution)/shard_map/attend/pallas_call | solution.py:201
  238.9 7.1 all-to-all-start.4
  246.6 9.2 fusion.50
  270.1 7.5 fusion.49
  277.6 11.3 %multiply_convert_fusion = (bf16[1024,2048]{1,0:T(8,128)(2,1)S(1)}, bf16[1024,2048]{1,0:T(8,128)(2,1)S(1)}, bf16[1024,2048]{1,0:T(8,128)(2,1)S(1)}) fusion(f32[1024,2048]{1,0:T(8,128)} %fusion.50, f32[1024,2048]{1,0:T(8,128)} %fusion.49, bf16[1024,768]{1,0:T(8,128)(2,1)S(1)} %multiply_convert_fusion.3, bf16[768,2048]{1,0:T(8,128)(2,1)} %all-gather.7.cloned.1.call-done), kind=kOutput, calls=%fused_computation | convolution fusion | flops 3252682752 | bytes 34078720 | tf_op jit(solution)/shard_map/dot_general | solution.py:446
  339.3 7.9 add_convert_fusion
  363.7 43.0 %attend_grad.3 = (bf16[16,384,128]{2,1,0:T(8,128)(2,1)}, bf16[16,256,128]{2,1,0:T(8,128)(2,1)}) custom-call(s32[33]{0:T(128)} %pad_add_fusion.3.info, s32[8]{0:T(128)} %copy-done.54, bf16[16,384,128]{2,1,0:T(8,128)(2,1)} %all-to-all-done.mine, bf16[16,384,128]{2,1,0:T(8,128)(2,1)} %collective-permute-done.3.other, ...), custom_call_target="tpu_custom_call" | custom-call | flops 32000000000 | bytes 10000000 | tf_op jit(solution)/shard_map/attend_grad/pallas_call | solution.py:298
  415.2 13.2 %collective-permute-done.15 = bf16[192,2048]{1,0:T(8,128)(2,1)} collective-permute-done((bf16[192,2048]{1,0:T(8,128)(2,1)}, bf16[192,2048]{1,0:T(8,128)(2,1)}, u32[]{:S(2)}, u32[]{:S(2)}) %collective-permute-start.15) | collective-permute-done | bytes 786464 | tf_op jit(solution)/shard_map/ppermute | solution.py:617
  441.0 43.0 %attend_grad.4 = (bf16[16,384,128]{2,1,0:T(8,128)(2,1)}, bf16[16,256,128]{2,1,0:T(8,128)(2,1)}) custom-call(s32[33]{0:T(128)} %pad_add_fusion.5.info, s32[8]{0:T(128)} %copy-done.54, bf16[16,384,128]{2,1,0:T(8,128)(2,1)} %copy-done.29, bf16[16,384,128]{2,1,0:T(8,128)(2,1)} %collective-permute-done.8.other, bf16[16,256,128]{2,1,0:T(8,128)(2,1)} %all-to-all-done.7.do_ref, ...), custom_call_target="tpu_custom_call" | custom-call | flops 32000000000 | bytes 10000000 | tf_op jit(solution)/shard_map/attend_grad/pallas_call | solution.py:298
  489.1 71.3 %all-reduce.16.cloned.1.call-done = (bf16[2,208,768]{2,1,0:T(8,128)(2,1)}, bf16[2,512,768]{2,1,0:T(8,128)(2,1)}) async-done(((bf16[2,208,768]{2,1,0:T(8,128)(2,1)}, bf16[2,512,768]{2,1,0:T(8,128)(2,1)}), (bf16[2,208,768]{2,1,0:T(8,128)(2,1)}, bf16[2,512,768]{2,1,0:T(8,128)(2,1)})) %all-reduce.16.cloned.1.call-update) | async-done | bytes 2211856 | tf_op jit(solution)/shard_map/psum | solution.py:637
  568.8 43.4 %attend_grad.5 = (bf16[16,384,128]{2,1,0:T(8,128)(2,1)}, bf16[16,256,128]{2,1,0:T(8,128)(2,1)}) custom-call(s32[33]{0:T(128)} %pad_add_fusion.6.info, s32[8]{0:T(128)} %copy-done.54, bf16[16,384,128]{2,1,0:T(8,128)(2,1)} %all-to-all-done.1.mine, bf16[16,384,128]{2,1,0:T(8,128)(2,1)} %collective-permute-done.9.other, ...), custom_call_target="tpu_custom_call" | custom-call | flops 32000000000 | bytes 10000000 | tf_op jit(solution)/shard_map/attend_grad/pallas_call | solution.py:298
  642.8 97.4 %all-reduce.14.cloned.1.call-done = (bf16[2,192,2048]{2,1,0:T(8,128)(2,1)}, bf16[2,192,2048]{2,1,0:T(8,128)(2,1)}) async-done(((bf16[2,192,2048]{2,1,0:T(8,128)(2,1)}, bf16[2,192,2048]{2,1,0:T(8,128)(2,1)}), (bf16[2,192,2048]{2,1,0:T(8,128)(2,1)}, bf16[2,192,2048]{2,1,0:T(8,128)(2,1)})) %all-reduce.14.cloned.1.call-update) | async-done | bytes 3145744 | tf_op jit(solution)/shard_map/psum | solution.py:637
  778.9 7.3 fusion.13
  790.1 75.6 %all-reduce.12.cloned.1.call-done = (bf16[2,192,768]{2,1,0:T(8,128)(2,1)}, bf16[2,192,768]{2,1,0:T(8,128)(2,1)}) async-done(((bf16[2,192,768]{2,1,0:T(8,128)(2,1)}, bf16[2,192,768]{2,1,0:T(8,128)(2,1)}), (bf16[2,192,768]{2,1,0:T(8,128)(2,1)}, bf16[2,192,768]{2,1,0:T(8,128)(2,1)})) %all-reduce.12.cloned.1.call-update) | async-done | bytes 1179664 | tf_op jit(solution)/shard_map/psum | solution.py:637
  883.1 86.2 %all-reduce.10.cloned.1.call-done = bf16[2,208,768]{2,1,0:T(8,128)(2,1)} async-done(((bf16[2,208,768]{2,1,0:T(8,128)(2,1)}), bf16[2,208,768]{2,1,0:T(8,128)(2,1)}) %all-reduce.10.cloned.1.call-update) | async-done | bytes 638992 | tf_op jit(solution)/shard_map/psum | solution.py:637
  (350 shorter events, 263.0 us)
Async XLA Ops:
  33.6 37.9 %all-to-all-start = ((bf16[16,384,128]{2,1,0:T(8,128)(2,1)}), bf16[16,384,128]{2,1,0:T(8,128)(2,1)}, u32[]{:S(2)}, u32[]{:S(2)}) async-start(bf16[16,384,128]{2,1,0:T(8,128)(2,1)} %bitcast.228), calls=%async_computation | async-start | bytes 3145728 | tf_op jit(solution)/shard_map/all_to_all | solution.py:566
  39.6 207.0 %all-gather.11.cloned.1.call-start = ((), (), s32[]{:S(2)}) async-start(), calls=%async_computation.13 | async-start | bytes 4718592 | tf_op jit(solution)/shard_map/all_gather | solution.py:520
  80.2 57.6 %all-to-all-start.2 = ((bf16[16,384,128]{2,1,0:T(8,128)(2,1)}), bf16[16,384,128]{2,1,0:T(8,128)(2,1)S(1)}, u32[]{:S(2)}, u32[]{:S(2)}) async-start(bf16[16,384,128]{2,1,0:T(8,128)(2,1)} %bitcast.227), calls=%async_computation.2 | async-start | bytes 3145728 | tf_op jit(solution)/shard_map/all_to_all | solution.py:566
  88.7 176.1 %all-gather.5.cloned.1.call-start = ((), (), s32[]{:S(2)}) async-start(), calls=%async_computation.10 | async-start | bytes 1769472 | tf_op jit(solution)/shard_map/all_gather | solution.py:520
  100.6 37.3 %collective-permute-start.5 = (bf16[384,384]{1,0:T(8,128)(2,1)}, bf16[384,384]{1,0:T(8,128)(2,1)S(1)}, u32[]{:S(2)}, u32[]{:S(2)}) collective-permute-start(bf16[384,384]{1,0:T(8,128)(2,1)} %collective-permute-done.4.refs_1_), channel_id=1, source_target_pairs={{0,2},{2,0},{4,6},{6,4},{8,10},{10,8},{12,14},{14,12},{16,18},{18,... | collective-permute-start | bytes 884744 | tf_op jit(solution)/shard_map/ppermute | solution.py:528
  145.8 45.4 %all-to-all-start.1 = ((bf16[16,384,128]{2,1,0:T(8,128)(2,1)}), bf16[16,384,128]{2,1,0:T(8,128)(2,1)}, u32[]{:S(2)}, u32[]{:S(2)}) async-start(bf16[16,384,128]{2,1,0:T(8,128)(2,1)} %bitcast.229), calls=%async_computation.1 | async-start | bytes 3145728 | tf_op jit(solution)/shard_map/all_to_all | solution.py:566
  152.3 117.8 %all-gather.9.cloned.1.call-start = ((), (), s32[]{:S(2)}) async-start(), calls=%async_computation.12 | async-start | bytes 4718592 | tf_op jit(solution)/shard_map/all_gather | solution.py:520
  193.3 45.5 %all-to-all-start.3 = ((bf16[16,256,128]{2,1,0:T(8,128)(2,1)}), bf16[16,256,128]{2,1,0:T(8,128)(2,1)S(1)}, u32[]{:S(2)}, u32[]{:S(2)}) async-start(bf16[16,256,128]{2,1,0:T(8,128)(2,1)} %pad_maximum_fusion.6), calls=%async_computation.3 | async-start | bytes 2097152 | tf_op jit(solution)/shard_map/all_to_all | solution.py:566
  200.2 77.4 %all-gather.7.cloned.1.call-start = ((), (), s32[]{:S(2)}) async-start(), calls=%async_computation.11 | async-start | bytes 4718592 | tf_op jit(solution)/shard_map/all_gather | solution.py:520
  295.0 55.2 %collective-permute-start.11 = (bf16[2,512,768]{2,1,0:T(8,128)(2,1)}, bf16[2,512,768]{2,1,0:T(8,128)(2,1)}, u32[]{:S(2)}, u32[]{:S(2)}) collective-permute-start(bf16[2,512,768]{2,1,0:T(8,128)(2,1)} %dynamic-slice_bitcast_fusion.2), channel_id=1, source_target_pairs={{0,2},{2,0},{4,6},{6,4},{8,10},{10,8},{12,14},{14,12},{16,18},{18,... | collective-permute-start | bytes 4718600 | tf_op jit(solution)/shard_map/ppermute | solution.py:617
  321.9 31.3 %collective-permute-start.12 = (bf16[2,192,2048]{2,1,0:T(8,128)(2,1)}, bf16[2,192,2048]{2,1,0:T(8,128)(2,1)}, u32[]{:S(2)}, u32[]{:S(2)}) collective-permute-start(bf16[2,192,2048]{2,1,0:T(8,128)(2,1)} %dynamic-slice_bitcast_fusion.1), channel_id=1, source_target_pairs={{0,2},{2,0},{4,6},{6,4},{8,10},{10,8},{12,14},{14,12},{16,18},{18,... | collective-permute-start | bytes 4718600 | tf_op jit(solution)/shard_map/ppermute | solution.py:617
  324.3 31.1 %collective-permute-start.13 = (bf16[2,192,2048]{2,1,0:T(8,128)(2,1)}, bf16[2,192,2048]{2,1,0:T(8,128)(2,1)}, u32[]{:S(2)}, u32[]{:S(2)}) collective-permute-start(bf16[2,192,2048]{2,1,0:T(8,128)(2,1)} %dynamic-slice_bitcast_fusion), channel_id=1, source_target_pairs={{0,2},{2,0},{4,6},{6,4},{8,10},{10,8},{12,14},{14,12},{16,18},{18,... | collective-permute-start | bytes 4718600 | tf_op jit(solution)/shard_map/ppermute | solution.py:617
  357.6 76.0 %all-to-all-start.7 = ((bf16[16,256,128]{2,1,0:T(8,128)(2,1)}), bf16[16,256,128]{2,1,0:T(8,128)(2,1)}, u32[]{:S(2)}, u32[]{:S(2)}) async-start(bf16[16,256,128]{2,1,0:T(8,128)(2,1)} %bitcast.238), calls=%async_computation.7 | async-start | bytes 2097152 | tf_op jit(solution)/shard_map/all_to_all | solution.py:566
  363.3 49.2 %collective-permute-start.17 = (bf16[512,768]{1,0:T(8,128)(2,1)}, bf16[512,768]{1,0:T(8,128)(2,1)}, u32[]{:S(2)}, u32[]{:S(2)}) collective-permute-start(bf16[512,768]{1,0:T(8,128)(2,1)} %dynamic-slice_bitcast_fusion.4), channel_id=1, source_target_pairs={{0,1},{1,0},{2,3},{3,2},{4,5},{5,4},{6,7},{7,6},{8,9},{9,8},{10,11... | collective-permute-start | bytes 2359304 | tf_op jit(solution)/shard_map/ppermute | solution.py:617
  412.2 71.7 %collective-permute-start.18 = (bf16[192,2048]{1,0:T(8,128)(2,1)}, bf16[192,2048]{1,0:T(8,128)(2,1)}, u32[]{:S(2)}, u32[]{:S(2)}) collective-permute-start(bf16[192,2048]{1,0:T(8,128)(2,1)} %dynamic-slice_bitcast_fusion.3), channel_id=1, source_target_pairs={{0,1},{1,0},{2,3},{3,2},{4,5},{5,4},{6,7},{7,6},{8,9},{9,8},{10,11... | collective-permute-start | bytes 2359304 | tf_op jit(solution)/shard_map/ppermute | solution.py:617
  433.6 130.2 %all-to-all-start.6 = ((bf16[16,384,128]{2,1,0:T(8,128)(2,1)}), bf16[16,384,128]{2,1,0:T(8,128)(2,1)S(1)}, u32[]{:S(2)}, u32[]{:S(2)}) async-start(bf16[16,384,128]{2,1,0:T(8,128)(2,1)} %pad_maximum_fusion), calls=%async_computation.6 | async-start | bytes 3145728 | tf_op jit(solution)/shard_map/all_to_all | solution.py:566
  440.4 120.0 %all-reduce.16.cloned.1.call-start = ((), (), s32[]{:S(2)}) async-start(), calls=%async_computation.17 | async-start | bytes 4423680 | tf_op jit(solution)/shard_map/psum | solution.py:637
  564.9 52.6 %all-to-all-start.8 = ((bf16[16,384,128]{2,1,0:T(8,128)(2,1)}), bf16[16,384,128]{2,1,0:T(8,128)(2,1)S(1)}, u32[]{:S(2)}, u32[]{:S(2)}) async-start(bf16[16,384,128]{2,1,0:T(8,128)(2,1)} %pad_maximum_fusion.1), calls=%async_computation.8 | async-start | bytes 3145728 | tf_op jit(solution)/shard_map/all_to_all | solution.py:566
  568.7 171.5 %all-reduce.14.cloned.1.call-start = ((), (), s32[]{:S(2)}) async-start(), calls=%async_computation.16 | async-start | bytes 6291456 | tf_op jit(solution)/shard_map/psum | solution.py:637
  628.1 125.9 %collective-permute-start.25 = (bf16[2,192,768]{2,1,0:T(8,128)(2,1)}, bf16[2,192,768]{2,1,0:T(8,128)(2,1)}, u32[]{:S(2)}, u32[]{:S(2)}) collective-permute-start(bf16[2,192,768]{2,1,0:T(8,128)(2,1)} %dynamic-slice_bitcast_fusion.8), channel_id=1, source_target_pairs={{0,2},{2,0},{4,6},{6,4},{8,10},{10,8},{12,14},{14,12},{16,18},{18,... | collective-permute-start | bytes 1769480 | tf_op jit(solution)/shard_map/ppermute | solution.py:617
  631.4 141.0 %all-to-all-start.9 = ((bf16[16,384,128]{2,1,0:T(8,128)(2,1)}), bf16[16,384,128]{2,1,0:T(8,128)(2,1)S(1)}, u32[]{:S(2)}, u32[]{:S(2)}) async-start(bf16[16,384,128]{2,1,0:T(8,128)(2,1)} %pad_maximum_fusion.2), calls=%async_computation.9 | async-start | bytes 3145728 | tf_op jit(solution)/shard_map/all_to_all | solution.py:566
  638.4 227.3 %all-reduce.12.cloned.1.call-start = ((), (), s32[]{:S(2)}) async-start(), calls=%async_computation.15 | async-start | bytes 2359296 | tf_op jit(solution)/shard_map/psum | solution.py:637
  772.3 196.9 %all-reduce.10.cloned.1.call-start = ((), (), s32[]{:S(2)}) async-start(), calls=%async_computation.14 | async-start | bytes 1277952 | tf_op jit(solution)/shard_map/psum | solution.py:637
  790.1 78.0 %collective-permute-start.21 = (bf16[2,208,768]{2,1,0:T(8,128)(2,1)}, bf16[2,208,768]{2,1,0:T(8,128)(2,1)}, u32[]{:S(2)}, u32[]{:S(2)}) collective-permute-start(bf16[2,208,768]{2,1,0:T(8,128)(2,1)} %dynamic-slice_bitcast_fusion.6), channel_id=1, source_target_pairs={{0,2},{2,0},{4,6},{6,4},{8,10},{10,8},{12,14},{14,12},{16,18},{18,... | collective-permute-start | bytes 1916936 | tf_op jit(solution)/shard_map/ppermute | solution.py:617
  (85 other events, 946.9 us)
Sparse Core Ops, SparseCore 0:
  49.2 45.6 all-gather.10
  138.1 23.7 all-gather.4
  163.4 44.9 all-gather.8
  209.8 44.9 all-gather.6
  445.1 115.2 all-reduce.15
  614.3 125.8 all-reduce.13
  772.4 93.1 all-reduce.11
  879.0 90.2 all-reduce.9
